TPU v7x, 128 devices: a whole 4x4x4 slice. The times are simulated.
128 devices in a mesh: ctx: 8 (over y, z_hi), chan: 16 (over x, z_lo, core).
Axes of the slice: x: 4, y: 4, z: 4 (z_hi: 2, z_lo: 2; z = z_hi * 2 + z_lo), core: 2. Of those that a mesh axis runs over, the one named last changes fastest.
Arguments:
- featurized: bfloat16 [16384, 3, 8192], P('ctx', None, 'chan'), may hold values from -6 to 6
- short_filter: float32 [3, 3, 8192], P(None, None, 'chan'), may hold values from -2.5 to 2.5
- decay_rate: float32 [512, 16], P('chan'), as said below
- residue: float32 [512, 16], P('chan'), may hold values from -2.5 to 2.5
- skip_gain: float32 [8192], P('chan'), may hold values from 0.25 to 1.5
- out_weight: bfloat16 [8192, 4096], P('chan'), may hold values from -0.0625 to 0.0625
Outputs:
- output: bfloat16 [16384, 4096], P(('ctx', 'chan'))
Inputs may be any that keep to these rules, and one draw needn't show every extreme that they name: `decay_rate`: each rate is at least 0.2 / 16384.
All inputs are finite; a program needn't handle non-finite values.
Results may differ from a plain program's by a relative error of at most 0.02.
Values may be sent and summed in bfloat16 or wider, within the bound.
A program may use at most 256 MiB of HBM per device.

v0:
```python
import jax
import jax.numpy as jnp
from jax import lax
from jax.sharding import Mesh
from jax.sharding import PartitionSpec as P

CHAN = ("chan_0", "chan_1", "chan_2")
CTX_CHAN = ("ctx", "chan_0", "chan_1", "chan_2")


def shifted(value, axis, steps):
    count = lax.axis_size(axis)
    first, last = (max(0, -steps), min(count, count - steps))
    return lax.ppermute(value, axis, [(source, source + steps) for source in range(first, last)])


def laid_out(pieces, dim):
    pieces = jnp.moveaxis(pieces, 0, dim)
    shape = pieces.shape
    return pieces.reshape(*shape[:dim], shape[dim] * shape[dim + 1], *shape[dim + 2 :])


def sent_to_all(shard, axis):
    peers = lax.axis_size(axis)
    return lax.all_to_all(
        jnp.broadcast_to(shard[None], (peers, *shard.shape)), axis, 0, 0, tiled=True
    )


def gathered_copies(shard, axis, dim):
    return laid_out(sent_to_all(shard, axis), dim)


def own_block_2(pieces, axes, turns):
    shape = [lax.axis_size(a) for a in axes]
    pieces = pieces.reshape(*shape, *pieces.shape[1:])
    pieces = pieces.transpose(*turns, *range(len(axes), pieces.ndim))
    pieces = pieces.reshape(-1, *pieces.shape[len(axes) :])
    for k in turns:
        pieces = lax.psum_scatter(pieces, axes[k], scatter_dimension=0, tiled=True)
    return pieces[0]


def split_up(shard, dim, peers):
    shape = shard.shape
    pieces = shard.reshape(*shape[:dim], peers, shape[dim] // peers, *shape[dim + 1 :])
    return jnp.moveaxis(pieces, dim, 0)


def summed_rows(shard, axes, turns, dim):
    peers = lax.axis_size(axes)
    return own_block_2(split_up(shard, dim, peers), axes, turns)


def own_block(local_filter, source_t, tile_count):
    filters, tok_rows = local_filter.shape
    group = source_t.shape[1]
    width = tok_rows // tile_count
    padded = jnp.concatenate([jnp.zeros((filters, width), jnp.float32), local_filter], axis=1)
    offsets = (
        jnp.arange(width, dtype=jnp.int32)[:, None]
        - jnp.arange(width, dtype=jnp.int32)[None, :]
        + width
    )
    tiles = source_t.reshape(filters, group, tile_count, width)
    summed = jnp.zeros((filters, group, tile_count, width), jnp.float32)
    for lag_tile in range(tile_count):
        segment = padded[:, lag_tile * width : lag_tile * width + 2 * width]
        toeplitz = jnp.take(segment, offsets, axis=1)
        product = jnp.einsum(
            "fts,fgps->fgpt",
            toeplitz,
            tiles[:, :, : tile_count - lag_tile],
            precision=lax.Precision.HIGHEST,
        )
        summed = summed.at[:, :, lag_tile:].add(product)
    return summed.reshape(filters, group, tok_rows)


def on_device(featurized, short_filter, decay_rate, residue, skip_gain, out_weight):
    tok_rows = featurized.shape[0]
    channels = featurized.shape[2]
    filters = decay_rate.shape[0]
    group = channels // filters
    rim_rows = shifted(featurized[tok_rows - 2 :], "ctx", 1)
    extended = jnp.concatenate([rim_rows, featurized], axis=0).astype(jnp.float32)
    shortened = (
        short_filter[0] * extended[2:]
        + short_filter[1] * extended[1:-1]
        + short_filter[2] * extended[:-2]
    )
    query_part = shortened[:, 0]
    gated = (shortened[:, 1] * shortened[:, 2]).astype(jnp.bfloat16)
    gated_float = gated.astype(jnp.float32)
    scaled = residue * jnp.sqrt(-jnp.expm1(-2.0 * decay_rate))
    positions = jnp.arange(tok_rows, dtype=jnp.float32)
    powers = jnp.exp(-decay_rate[:, :, None] * positions)
    tails = jnp.exp(-decay_rate[:, :, None] * (tok_rows - positions))
    signals_t = gated_float.reshape(tok_rows, filters, group).transpose(1, 2, 0)
    local_state = jnp.einsum("fmt,fgt->fmg", tails, signals_t, precision=lax.Precision.HIGHEST)
    own_index = lax.axis_index("ctx")
    piece = gathered_copies(local_state[None].astype(jnp.bfloat16), "ctx", 0).astype(jnp.float32)
    lags = own_index - 1 - jnp.arange(piece.shape[0], dtype=jnp.int32)
    spans = jnp.maximum(lags, 0).astype(jnp.float32) * tok_rows
    weights = jnp.where(
        lags[:, None, None] >= 0, jnp.exp(-decay_rate[None] * spans[:, None, None]), 0.0
    )
    carried = jnp.zeros_like(local_state) + jnp.einsum(
        "kfm,kfmg->fmg", weights, piece, precision=lax.Precision.HIGHEST
    )
    far_part = jnp.einsum(
        "fmt,fmg->fgt", scaled[:, :, None] * powers, carried, precision=lax.Precision.HIGHEST
    )
    local_filter = jnp.einsum("fm,fmt->ft", scaled, powers, precision=lax.Precision.HIGHEST)
    tile_count = tok_rows // 256
    near_part = own_block(local_filter, signals_t, tile_count)
    long_conv = (near_part + far_part).transpose(2, 0, 1).reshape(tok_rows, channels)
    mixed_rows = (query_part * (long_conv + skip_gain * gated_float)).astype(jnp.bfloat16)
    return (
        summed_rows(
            jnp.dot(mixed_rows, out_weight, preferred_element_type=jnp.float32).astype(
                jnp.bfloat16
            ),
            CHAN,
            (2, 0, 1),
            0,
        )
        .astype(jnp.float32)
        .astype(jnp.bfloat16)
    )


def solution(mesh):
    finer = Mesh(
        mesh.devices.reshape(mesh.shape["ctx"], 4, 2, 2), ("ctx", "chan_0", "chan_1", "chan_2")
    )
    placed = (
        P("ctx", None, CHAN),
        P(None, None, CHAN),
        P(CHAN, None),
        P(CHAN, None),
        P(CHAN),
        P(CHAN, None),
    )
    return jax.shard_map(
        on_device, mesh=finer, in_specs=placed, out_specs=P(CTX_CHAN, None), check_vma=False
    )
```

profile of v0, /device:TPU:1, one launch (start us, length us, event | category | flops | bytes accessed | tf_op | source)
XLA Modules:
  0.0 2365.2 jit_solution(8274057639329485816)
XLA Ops:
  22.9 9.4 copy.56
  32.3 215.6 %gather_fusion = f32[65536,32]{1,0:T(8,128)} fusion(f32[32,512]{0,1:T(8,128)S(1)} %get-tuple-element.121, s32[65536]{0:T(1024)S(1)} %broadcast_clamp_fusion), kind=kCustom, calls=%fused_computation.clone | custom fusion | bytes 17039360 | tf_op jit(solution)/shard_map/jit(_take)/gather | solution.py:69
  247.9 22.2 copy.58
  270.1 215.6 %gather_fusion.1 = f32[65536,32]{1,0:T(8,128)} fusion(f32[32,512]{0,1:T(8,128)S(1)} %get-tuple-element.120, s32[65536]{0:T(1024)S(1)} %broadcast_clamp_fusion), kind=kCustom, calls=%fused_computation.1.clone | custom fusion | bytes 17039360 | tf_op jit(solution)/shard_map/jit(_take)/gather | solution.py:69
  485.6 22.2 copy.60
  507.8 215.6 %gather_fusion.2 = f32[65536,32]{1,0:T(8,128)} fusion(f32[32,512]{0,1:T(8,128)S(1)} %get-tuple-element.119, s32[65536]{0:T(1024)S(1)} %broadcast_clamp_fusion), kind=kCustom, calls=%fused_computation.2.clone | custom fusion | bytes 17039360 | tf_op jit(solution)/shard_map/jit(_take)/gather | solution.py:69
  723.4 22.2 copy.63
  745.5 215.6 %gather_fusion.3 = f32[65536,32]{1,0:T(8,128)} fusion(f32[32,512]{0,1:T(8,128)S(1)} %get-tuple-element.118, s32[65536]{0:T(1024)S(1)} %broadcast_clamp_fusion), kind=kCustom, calls=%fused_computation.3.clone | custom fusion | bytes 17039360 | tf_op jit(solution)/shard_map/jit(_take)/gather | solution.py:69
  961.1 22.2 copy.66
  983.2 215.6 %gather_fusion.4 = f32[65536,32]{1,0:T(8,128)} fusion(f32[32,512]{0,1:T(8,128)S(1)} %get-tuple-element.117, s32[65536]{0:T(1024)S(1)} %broadcast_clamp_fusion), kind=kCustom, calls=%fused_computation.4.clone | custom fusion | bytes 17039360 | tf_op jit(solution)/shard_map/jit(_take)/gather | solution.py:69
  1198.8 22.2 copy.69
  1221.0 215.6 %gather_fusion.5 = f32[65536,32]{1,0:T(8,128)} fusion(f32[32,512]{0,1:T(8,128)S(1)} %copy-done.2, s32[65536]{0:T(1024)S(1)} %broadcast_clamp_fusion), kind=kCustom, calls=%fused_computation.5.clone | custom fusion | bytes 17039360 | tf_op jit(solution)/shard_map/jit(_take)/gather | solution.py:69
  1436.6 22.2 copy.72
  1458.7 215.6 %gather_fusion.6 = f32[65536,32]{1,0:T(8,128)} fusion(f32[32,512]{0,1:T(8,128)S(1)} %copy-done.1, s32[65536]{0:T(1024)S(1)} %broadcast_clamp_fusion), kind=kCustom, calls=%fused_computation.6.clone | custom fusion | bytes 17039360 | tf_op jit(solution)/shard_map/jit(_take)/gather | solution.py:69
  1674.3 22.1 copy.75
  1696.4 215.6 %gather_fusion.7 = f32[65536,32]{1,0:T(8,128)} fusion(f32[32,512]{0,1:T(8,128)S(1)} %copy-done, s32[65536]{0:T(1024)S(1)} %broadcast_clamp_fusion), kind=kCustom, calls=%fused_computation.7.clone | custom fusion | bytes 17039360 | tf_op jit(solution)/shard_map/jit(_take)/gather | solution.py:69
  1912.0 22.2 copy.78
  1940.0 11.6 fusion
  1970.9 8.6 fusion.14
  1979.5 10.0 fusion.12
  2003.9 23.7 %scatter-add.24 = f32[32,16,8,256]{3,2,1,0:T(8,128)} dynamic-update-slice(f32[32,16,8,256]{3,2,1,0:T(8,128)} %copy-done.3, f32[32,16,7,256]{3,2,1,0:T(8,128)} %copy-done.4, s32[]{:T(128)} %constant.252.clone.1, s32[]{:T(128)} %constant.252.clone.1, s32[]{:T(128)} %constant.253.clone.1, s32[]{:T(128)} %constant.252.clone.1) | dynamic-update-slice | bytes 7340036 | tf_op jit(solution)/shard_map/scatter-add | solution.py:76
  2027.6 8.5 fusion.8
  2040.7 23.6 scatter-add.25
  2072.3 23.8 %scatter-add.26 = f32[32,16,8,256]{3,2,1,0:T(8,128)} dynamic-update-slice(f32[32,16,8,256]{3,2,1,0:T(8,128)} %scatter-add.25, f32[32,16,5,256]{3,2,1,0:T(8,128)} %slice_add_fusion, s32[]{:T(128)} %constant.252.clone.1, s32[]{:T(128)} %constant.252.clone.1, s32[]{:T(128)} %constant.255.clone.1, s32[]{:T(128)} %constant.252.clone.1) | dynamic-update-slice | bytes 5242884 | tf_op jit(solution)/shard_map/scatter-add | solution.py:76
  2102.1 8.2 fusion.4
  2116.9 22.6 scatter-add.30
  2150.3 12.3 scatter-add.34
  2179.9 12.6 convolution_convert_fusion
  2192.5 14.0 copy.82
  2206.6 31.3 %reduce-scatter.4.cloned.1.call-done = bf16[8,128,4096]{2,1,0:T(8,128)(2,1)} async-done(((bf16[16,128,4096]{2,1,0:T(8,128)(2,1)}), bf16[8,128,4096]{2,1,0:T(8,128)(2,1)}) %reduce-scatter.4.cloned.1.call-update) | async-done | bytes 8388624 | tf_op jit(solution)/shard_map/reduce_scatter | solution.py:40
  2238.0 84.0 %reduce-scatter.6.cloned.1.call-done = bf16[2,128,4096]{2,1,0:T(8,128)(2,1)} async-done(((bf16[8,128,4096]{2,1,0:T(8,128)(2,1)}), bf16[2,128,4096]{2,1,0:T(8,128)(2,1)}) %reduce-scatter.6.cloned.1.call-update) | async-done | bytes 2097168 | tf_op jit(solution)/shard_map/reduce_scatter | solution.py:40
  2322.0 36.5 %reduce-scatter.8.cloned.1.call-done = bf16[1,128,4096]{2,1,0:T(8,128)(2,1)} async-done(((bf16[2,128,4096]{2,1,0:T(8,128)(2,1)}), bf16[1,128,4096]{2,1,0:T(8,128)(2,1)}) %reduce-scatter.8.cloned.1.call-update) | async-done | bytes 1048592 | tf_op jit(solution)/shard_map/reduce_scatter | solution.py:40
  (108 shorter events, 108.9 us)
Async XLA Ops:
  8.3 1926.0 %collective-permute-start = (bf16[2,3,512]{0,2,1:T(8,128)(2,1)}, bf16[2,3,512]{0,2,1:T(8,128)(2,1)}, u32[]{:S(2)}, u32[]{:S(2)}) collective-permute-start(bf16[2,3,512]{0,2,1:T(8,128)(2,1)} %copy.55), channel_id=1, source_target_pairs={{0,16},{16,32},{32,48},{48,64},{64,80},{80,96},{96,112},{1,17},{17... | collective-permute-start | bytes 18440 | tf_op jit(solution)/shard_map/ppermute | solution.py:14
  18.2 1.9 copy-start.13
  18.2 3.3 copy-start.11
  1198.8 22.2 copy-start.2
  1436.6 22.2 copy-start.1
  1674.3 22.1 copy-start
  1912.0 22.2 copy-start.10
  1934.3 5.7 copy-start.15
  1934.3 5.7 copy-start.16
  1934.3 5.7 copy-start.17
  1956.5 4.4 copy-start.12
  1956.5 4.4 copy-start.18
  1958.3 12.5 copy-start.6
  1967.4 200.2 %all-to-all-start = ((bf16[8,2,4096]{2,1,0:T(2,128)(2,1)}), bf16[8,2,4096]{2,1,0:T(2,128)(2,1)S(1)}, u32[]{:S(2)}, u32[]{:S(2)}) async-start(bf16[8,2,4096]{2,1,0:T(2,128)(2,1)} %reshape.464), calls=%async_computation | async-start | bytes 262144 | tf_op jit(solution)/shard_map/all_to_all | solution.py:25
  1970.8 267.1 %reduce-scatter.4.cloned.1.call-start = ((), (), s32[]{:S(2)}) async-start(), calls=%async_computation.4 | async-start | bytes 25165824 | tf_op jit(solution)/shard_map/reduce_scatter | solution.py:40
  1979.4 10.1 copy-start.3
  1979.5 14.2 slice-start.2
  1979.5 14.2 slice-start.3
  1993.6 5.1 copy-start.4
  2027.6 8.5 copy-start.5
  2096.1 6.0 copy-start.7
  2096.1 15.8 slice-start
  2102.1 9.8 slice-start.1
  2110.3 1.6 copy-start.8
  2139.5 2.4 copy-start.9
  2162.7 5.5 copy-start.14
  2168.2 5.9 copy-start.19
  2174.0 5.9 copy-start.20
  2206.6 115.3 %reduce-scatter.6.cloned.1.call-start = ((), (), s32[]{:S(2)}) async-start(), calls=%async_computation.5 | async-start | bytes 10485760 | tf_op jit(solution)/shard_map/reduce_scatter | solution.py:40
  2237.9 120.5 %reduce-scatter.8.cloned.1.call-start = ((), (), s32[]{:S(2)}) async-start(), calls=%async_computation.6 | async-start | bytes 3145728 | tf_op jit(solution)/shard_map/reduce_scatter | solution.py:40
Sparse Core Ops, SparseCore 0:
  2206.7 31.1 reduce-scatter.3
  2240.4 81.5 reduce-scatter.5
  2324.3 34.1 reduce-scatter.7
where the time goes:
time: 2370 us
  local copies, waits for them, and re-layouts  2050 us (86%)
  waiting for transfers between devices  152 us (6%)
  matrix products  82.6 us (3%)
  other arithmetic  56.7 us (2%)
    gather x16, local copies, waits for them, and re-layouts, own_block(): toeplitz = jnp.take(segment, offsets, axis=1)  1900 us
    reduce_scatter x3, waiting for transfers between devices, own_block_2(): pieces = lax.psum_scatter(pieces, axes[k], scatter_dimension=0, tiled=True)  152 us
    scatter-add x5, local copies, waits for them, and re-layouts, own_block(): summed = summed.at[:, :, lag_tile:].add(product)  106 us
    dot_general x8, matrix products, own_block(): jnp.einsum('fts,fgps->fgpt', toeplitz, tiles[:, :, :tile_count - lag_tile...  60.9 us
  transfers between devices with their start and end apart: 5, of which 3 were waited for; matrix products, arithmetic and copies ran while one was open for 89% of the time, Pallas kernels for 0%

commit v1 on v0

v1 whole, which is shorter than its diff:
```python
import jax
import jax.numpy as jnp
from jax import lax
from jax.experimental import pallas as pl
from jax.experimental.pallas import tpu as pltpu
from jax.sharding import Mesh
from jax.sharding import PartitionSpec as P

CHAN = ("chan_0", "chan_1", "chan_2")
CTX_CHAN = ("ctx", "chan_0", "chan_1", "chan_2")
MESH = pl.DeviceIdType.MESH
F32 = jnp.float32
BF16 = jnp.bfloat16
LANES = 128
STEP = 128
GROUP = 16
PACK = LANES // GROUP
MODES = 16
STRIP = 32
RIM = 16


def swapped(parts, lane_group):
    parts = list(parts)
    for bit in (1, 2, 4):
        low = (lane_group & bit) == 0
        for k in range(PACK):
            if k & bit == 0:
                a, b = parts[k], parts[k | bit]
                parts[k] = jnp.where(low, a, pltpu.roll(b, bit * GROUP, 1))
                parts[k | bit] = jnp.where(low, pltpu.roll(a, LANES - bit * GROUP, 1), b)
    return parts


def hi_lo(value):
    hi = value.astype(BF16).astype(F32)
    return hi, value - hi


def chunk_scan(state, rate, lane):
    width = state.shape[1]
    hop = 1
    while hop * GROUP < width:
        decay = jnp.exp(rate * (-float(hop * STEP)))
        moved = pltpu.roll(state, hop * GROUP, 1)
        state = state + jnp.where(lane >= hop * GROUP, decay * moved, 0.0)
        hop *= 2
    return state


def conv_kernel(
    feat_hbm,
    taps_ref,
    rate_row_ref,
    scale_row_ref,
    rate_ref,
    scale_ref,
    rate_chan_ref,
    skip_ref,
    mixed_ref,
    feat,
    rim,
    gated,
    query,
    source,
    left,
    local,
    total,
    totals,
    result,
    load_sem,
    rim_sem,
    sum_send,
    sum_recv,
):
    tokens, channels = feat.shape[1], feat.shape[2]
    chunks = tokens // STEP
    blocks = channels // LANES
    width = chunks * GROUP
    halves = width // LANES
    ctx = lax.axis_index("ctx")
    peers = lax.axis_size("ctx")

    loads = []
    for v in range(blocks):
        at = pl.ds(v * LANES, LANES)
        copy = pltpu.make_async_copy(feat_hbm.at[:, :, at], feat.at[:, :, at], load_sem.at[v])
        copy.start()
        loads.append(copy)

    barrier = pltpu.get_barrier_semaphore()
    for d in range(1, peers):
        pl.semaphore_signal(
            barrier, inc=1, device_id={"ctx": lax.rem(ctx + d, peers)}, device_id_type=MESH
        )
    pl.semaphore_wait(barrier, peers - 1)
    rim_copy = pltpu.make_async_remote_copy(
        src_ref=feat_hbm.at[:, pl.ds(tokens - RIM, RIM), :],
        dst_ref=rim,
        send_sem=rim_sem.at[0],
        recv_sem=rim_sem.at[1],
        device_id={"ctx": lax.rem(ctx + 1, peers)},
        device_id_type=MESH,
    )
    rim_copy.start()

    lane = lax.broadcasted_iota(jnp.int32, (1, LANES), 1)
    lane_group = lane // GROUP
    lane_wide = lax.broadcasted_iota(jnp.int32, (MODES, width), 1)
    lane_mode = lax.broadcasted_iota(jnp.int32, (MODES, LANES), 1)
    source[:, STEP + 3 * MODES :, :] = jnp.zeros(
        (source.shape[0], source.shape[1] - STEP - 3 * MODES, width), BF16
    )

    row = lax.broadcasted_iota(jnp.int32, (STEP, LANES), 0)
    col = lax.broadcasted_iota(jnp.int32, (STEP, LANES), 1)
    after = (row + 1).astype(F32)
    back = lax.rem(STEP - lane_mode, STEP).astype(F32)
    ahead = (STEP - 1 - lane_mode).astype(F32)

    def build(f, carry):
        first = jnp.sum(
            scale_ref[f] * jnp.exp(-rate_ref[f] * back), axis=0, keepdims=True
        )
        turned = pltpu.roll(
            jnp.broadcast_to(first, (STEP, LANES)), 0, 1, stride=1, stride_axis=0
        )
        left[f, :, :LANES] = jnp.where(col <= row, turned, 0.0).astype(BF16)
        rate = rate_row_ref[pl.ds(f, 1), :]
        scale = scale_row_ref[pl.ds(f, 1), :]
        hi, lo = hi_lo(scale * jnp.exp(-rate * after))
        second = (col >= MODES) & (col < 2 * MODES)
        left[f, :, LANES:] = jnp.where(second, lo, hi).astype(BF16)
        return carry

    for copy in loads:
        copy.wait()
    rim_copy.wait()

    def chunk_of(v, c):
        at = pl.ds(pl.multiple_of(v * LANES, LANES), LANES)
        here = pl.ds(pl.multiple_of(c * STEP, STEP), STEP)
        before = pl.ds(pl.multiple_of(jnp.maximum(c * STEP - RIM, 0), RIM), RIM)
        parts = []
        for i in range(3):
            earlier = feat[i, before, at].astype(F32)
            outside = jnp.where(ctx > 0, rim[i, :, at].astype(F32), 0.0)
            earlier = jnp.where(c > 0, earlier, outside)
            rows = jnp.concatenate([earlier, feat[i, here, at].astype(F32)], axis=0)
            tap = taps_ref[:, i, at]
            value = (
                tap[0:1] * rows[RIM:]
                + tap[1:2] * pltpu.roll(rows, 1, 0)[RIM:]
                + tap[2:3] * pltpu.roll(rows, 2, 0)[RIM:]
            )
            parts.append(value)
        query[here, at] = parts[0]
        gated[c] = (parts[1] * parts[2]).astype(BF16).astype(F32)

    def block_in(v, carry):
        at = pl.ds(pl.multiple_of(v * LANES, LANES), LANES)

        def one_chunk(c, inner):
            chunk_of(v, c)
            return inner

        lax.fori_loop(0, chunks, one_chunk, 0)

        def one_strip(s, inner):
            rows = pl.ds(pl.multiple_of(s * STRIP, STRIP), STRIP)
            for h in range(halves):
                parts = swapped([gated[h * PACK + k, rows, :] for k in range(PACK)], lane_group)
                for g in range(PACK):
                    source[v * PACK + g, rows, h * LANES : (h + 1) * LANES] = parts[g].astype(BF16)
            return inner

        lax.fori_loop(0, STEP // STRIP, one_strip, 0)
        packed = jnp.zeros((MODES, LANES), F32)
        for g in range(PACK):
            f = v * PACK + g
            rate = rate_ref[f]
            hi, lo = hi_lo(jnp.exp(-rate * ahead))
            weight = jnp.concatenate([hi, lo], axis=0).astype(BF16)
            product = jnp.dot(weight, source[f, :STEP, :], preferred_element_type=F32)
            ends = product[:MODES] + product[MODES:]
            local[f] = ends
            summed = chunk_scan(ends, jnp.concatenate([rate] * halves, axis=1), lane_wide)
            last = summed[:, width - LANES :]
            last = pltpu.roll(last, (g * GROUP + GROUP) % LANES, 1)
            packed = jnp.where(lane_group == g, last, packed)
        total[:, at] = packed
        return carry

    lax.fori_loop(0, blocks, block_in, 0)

    sums = []
    for d in range(1, peers):
        copy = pltpu.make_async_remote_copy(
            src_ref=total,
            dst_ref=totals.at[d - 1],
            send_sem=sum_send.at[d - 1],
            recv_sem=sum_recv.at[d - 1],
            device_id={"ctx": lax.rem(ctx + d, peers)},
            device_id_type=MESH,
        )
        copy.start()
        sums.append(copy)
    lax.fori_loop(0, left.shape[0], build, 0)
    for copy in sums:
        copy.wait()
    carried = jnp.zeros((MODES, channels), F32)
    for d in range(1, peers):
        weight = jnp.exp(rate_chan_ref[...] * (-float((d - 1) * tokens)))
        carried = carried + jnp.where(ctx >= d, weight * totals[d - 1], 0.0)
    total[...] = carried

    def block_out(v, carry):
        at = pl.ds(pl.multiple_of(v * LANES, LANES), LANES)
        incoming = total[:, at]
        for g in range(PACK):
            f = v * PACK + g
            entry = pltpu.roll(incoming, (LANES - g * GROUP) % LANES, 1)
            entry = jnp.concatenate([entry] * halves, axis=1)
            states = jnp.where(lane_wide < GROUP, entry, pltpu.roll(local[f], GROUP, 1))
            states = chunk_scan(
                states, jnp.concatenate([rate_ref[f]] * halves, axis=1), lane_wide
            )
            hi, lo = hi_lo(states)
            source[f, STEP : STEP + 3 * MODES, :] = jnp.concatenate([hi, hi, lo], axis=0).astype(
                BF16
            )
            out = jnp.dot(left[f], source[f], preferred_element_type=F32)
            result[g] = out + skip_ref[pl.ds(f, 1), :] * source[f, :STEP, :].astype(F32)

        def one_strip(s, inner):
            rows = pl.ds(pl.multiple_of(s * STRIP, STRIP), STRIP)
            for h in range(halves):
                parts = swapped(
                    [result[g, rows, h * LANES : (h + 1) * LANES] for g in range(PACK)],
                    lane_group,
                )
                for k in range(PACK):
                    here = pl.ds(
                        pl.multiple_of((h * PACK + k) * STEP + s * STRIP, STRIP), STRIP
                    )
                    mixed_ref[here, at] = (query[here, at] * parts[k]).astype(BF16)
            return inner

        lax.fori_loop(0, STEP // STRIP, one_strip, 0)
        return carry

    lax.fori_loop(0, blocks, block_out, 0)


def convolved(featurized, short_filter, decay_rate, residue, skip_gain):
    tokens, _, channels = featurized.shape
    filters = decay_rate.shape[0]
    chunks = tokens // STEP
    width = chunks * GROUP
    peers = lax.axis_size("ctx")
    scaled = residue * jnp.sqrt(-jnp.expm1(-2.0 * decay_rate))
    none = jnp.zeros((filters, LANES - 3 * MODES), F32)
    rate_row = jnp.concatenate([decay_rate] * 3 + [none], axis=1)
    scale_row = jnp.concatenate([scaled] * 3 + [none], axis=1)
    rate = jnp.broadcast_to(decay_rate[:, :, None], (filters, MODES, LANES))
    scale = jnp.broadcast_to(scaled[:, :, None], (filters, MODES, LANES))
    rate_chan = jnp.repeat(decay_rate.T, GROUP, axis=1)
    skip = jnp.tile(skip_gain.reshape(filters, GROUP), (1, chunks))
    vmem = pl.BlockSpec(memory_space=pltpu.VMEM)
    return pl.pallas_call(
        conv_kernel,
        out_shape=jax.ShapeDtypeStruct((tokens, channels), BF16),
        in_specs=[pl.BlockSpec(memory_space=pl.ANY)] + [vmem] * 7,
        out_specs=vmem,
        scratch_shapes=[
            pltpu.VMEM((3, tokens, channels), BF16),
            pltpu.VMEM((3, RIM, channels), BF16),
            pltpu.VMEM((chunks, STEP, LANES), F32),
            pltpu.VMEM((tokens, channels), F32),
            pltpu.VMEM((filters, 2 * STEP, width), BF16),
            pltpu.VMEM((filters, STEP, 2 * LANES), BF16),
            pltpu.VMEM((filters, MODES, width), F32),
            pltpu.VMEM((MODES, channels), F32),
            pltpu.VMEM((peers - 1, MODES, channels), F32),
            pltpu.VMEM((PACK, STEP, width), F32),
            pltpu.SemaphoreType.DMA((channels // LANES,)),
            pltpu.SemaphoreType.DMA((2,)),
            pltpu.SemaphoreType.DMA((peers - 1,)),
            pltpu.SemaphoreType.DMA((peers - 1,)),
        ],
        compiler_params=pltpu.CompilerParams(
            collective_id=0, has_side_effects=True, vmem_limit_bytes=48 * 2**20
        ),
        name="conv",
    )(
        featurized.transpose(1, 0, 2),
        short_filter,
        rate_row,
        scale_row,
        rate,
        scale,
        rate_chan,
        skip,
    )


TILE = 256


def project_kernel(
    mixed_hbm,
    weight_hbm,
    out_ref,
    mixed,
    weight,
    z_send,
    z_recv,
    far_send,
    far_recv,
    near_send,
    near_recv,
    far2_send,
    far2_recv,
    near2_send,
    near2_recv,
    turn_send,
    turn_recv,
    held,
    last_send,
    last_recv,
    load_sem,
    send_sem,
    recv_sem,
):
    depth = mixed_hbm.shape[1]
    cols = weight.shape[1]
    half = cols // 2
    quarter = cols // 4
    block = mixed_hbm.shape[0] // 4
    sub = block // 2
    own = sub // 2
    x = lax.axis_index("chan_0")
    z = lax.axis_index("chan_1")
    core = lax.axis_index("chan_2")
    right, far, lefts = lax.rem(x + 1, 4), lax.rem(x + 2, 4), lax.rem(x + 3, 4)
    to_right, to_left = {"chan_0": right}, {"chan_0": lefts}
    to_z, to_core = {"chan_1": 1 - z}, {"chan_2": 1 - core}
    order = (far, right, lefts, x)

    used = []

    def sent(src, dst, to):
        k = len(used)
        copy = pltpu.make_async_remote_copy(
            src_ref=src,
            dst_ref=dst,
            send_sem=send_sem.at[k],
            recv_sem=recv_sem.at[k],
            device_id=to,
            device_id_type=MESH,
        )
        copy.start()
        used.append(copy)
        return copy

    my_cols = pl.ds(pl.multiple_of(core * cols, cols), cols)
    other_cols = pl.ds(pl.multiple_of((1 - core) * cols, cols), cols)
    load = pltpu.make_async_copy(
        weight_hbm.at[:, my_cols], weight.at[pl.ds(0, depth), :], load_sem.at[0]
    )
    load.start()
    loads = []
    for k, at in enumerate(order):
        rows = pl.ds(pl.multiple_of(at * block, block), block)
        copy = pltpu.make_async_copy(
            mixed_hbm.at[rows, :], mixed.at[rows, pl.ds(0, depth)], load_sem.at[1 + k]
        )
        copy.start()
        loads.append(copy)

    barrier = pltpu.get_barrier_semaphore()
    for to in (to_right, to_left, to_z, to_core):
        pl.semaphore_signal(barrier, inc=1, device_id=to, device_id_type=MESH)
    pl.semaphore_wait(barrier, 4)

    passed = []
    for k, at in enumerate(order):
        rows = pl.ds(pl.multiple_of(at * block, block), block)
        if k == 1:
            weight_copy = sent(
                weight_hbm.at[:, other_cols], weight.at[pl.ds(depth, depth), :], to_core
            )
        passed.append(
            sent(mixed_hbm.at[rows, :], mixed.at[rows, pl.ds(depth, depth)], to_core)
        )

    def tiles(token, rows, first, count, store):
        wide = count // TILE

        def one(n, carry):
            i, j = n // wide, lax.rem(n, wide)
            r = pl.multiple_of(i * sub, sub)
            c = pl.multiple_of(j * TILE, TILE)
            value = jnp.dot(
                mixed[pl.ds(pl.multiple_of(token + r, sub), sub), :],
                weight[:, pl.ds(pl.multiple_of(first + c, TILE), TILE)],
                preferred_element_type=F32,
            )
            store(pl.ds(r, sub), pl.ds(c, TILE), value)
            return carry

        lax.fori_loop(0, (rows // sub) * wide, one, 0)

    def start_of(at):
        return at * block

    def plain(dst, extra=()):
        def store(r, c, value):
            for e in extra:
                value = value + e[r, c].astype(F32)
            dst[r, c] = value.astype(BF16)

        return store

    mine, others = z * sub, (1 - z) * sub

    def z_first(k):
        at = order[k]
        tiles(start_of(at) + others, sub, half, half, plain(z_send.at[k]))
        return sent(z_send.at[k], z_recv.at[k], to_z)

    load.wait()
    weight_copy.wait_recv()
    loads[0].wait()
    passed[0].wait_recv()
    zs = [z_first(0)]
    fars = []
    for s, to in ((0, to_right), (1, to_left)):
        tiles(start_of(far), block, s * quarter, quarter, plain(far_send.at[s]))
        fars.append(sent(far_send.at[s], far_recv.at[s], to))

    loads[1].wait()
    passed[1].wait_recv()
    zs.append(z_first(1))
    loads[2].wait()
    passed[2].wait_recv()
    zs.append(z_first(2))
    nears = {}
    for s, at, to in ((0, right, to_right), (1, lefts, to_left)):
        side = 1 - s
        tiles(start_of(at), block, side * quarter, quarter, plain(near_send.at[s, side]))
        nears[s, side] = sent(near_send.at[s, side], near_recv.at[s, side], to)
    loads[3].wait()
    passed[3].wait_recv()
    zs.append(z_first(3))
    for s, at, to in ((0, right, to_right), (1, lefts, to_left)):
        fars[s].wait_recv()
        tiles(
            start_of(at), block, s * quarter, quarter, plain(near_send.at[s, s], (far_recv.at[s],))
        )
        nears[s, s] = sent(near_send.at[s, s], near_recv.at[s, s], to)

    zs[0].wait_recv()
    fars2 = []
    for s, to in ((0, to_right), (1, to_left)):
        at = pl.ds(s * quarter, quarter)
        tiles(
            start_of(far) + mine,
            sub,
            half + s * quarter,
            quarter,
            plain(far2_send.at[s], (z_recv.at[0, :, at],)),
        )
        fars2.append(sent(far2_send.at[s], far2_recv.at[s], to))
    nears2 = {}
    for s, at, to in ((0, right, to_right), (1, lefts, to_left)):
        zs[1 + s].wait_recv()
        side = 1 - s
        piece = pl.ds(side * quarter, quarter)
        tiles(
            start_of(at) + mine,
            sub,
            half + side * quarter,
            quarter,
            plain(near2_send.at[s, side], (z_recv.at[1 + s, :, piece],)),
        )
        nears2[s, side] = sent(near2_send.at[s, side], near2_recv.at[s, side], to)
    for s, at, to in ((0, right, to_right), (1, lefts, to_left)):
        fars2[s].wait_recv()
        piece = pl.ds(s * quarter, quarter)
        tiles(
            start_of(at) + mine,
            sub,
            half + s * quarter,
            quarter,
            plain(near2_send.at[s, s], (z_recv.at[1 + s, :, piece], far2_recv.at[s])),
        )
        nears2[s, s] = sent(near2_send.at[s, s], near2_recv.at[s, s], to)

    for copy in nears.values():
        copy.wait_recv()
    for side in (0, 1):
        piece = pl.ds(side * quarter, quarter)
        away = pl.ds(pl.multiple_of(others, sub), sub)
        tiles(
            start_of(x) + others,
            sub,
            side * quarter,
            quarter,
            plain(
                turn_send.at[:, piece],
                (near_recv.at[0, side, away], near_recv.at[1, side, away]),
            ),
        )
    turn = sent(turn_send, turn_recv, to_z)

    def kept(offset, extra):
        def store(r, c, value):
            for e in extra:
                value = value + e[r, c].astype(F32)
            held[r, pl.ds(pl.multiple_of(offset + c.start, TILE), TILE)] = value

        return store

    for side in (0, 1):
        here = pl.ds(pl.multiple_of(mine, sub), sub)
        tiles(
            start_of(x) + mine,
            sub,
            side * quarter,
            quarter,
            kept(side * quarter, (near_recv.at[0, side, here], near_recv.at[1, side, here])),
        )
    zs[3].wait_recv()
    for copy in nears2.values():
        copy.wait_recv()
    for side in (0, 1):
        piece = pl.ds(side * quarter, quarter)
        tiles(
            start_of(x) + mine,
            sub,
            half + side * quarter,
            quarter,
            kept(
                half + side * quarter,
                (z_recv.at[3, :, piece], near2_recv.at[0, side], near2_recv.at[1, side]),
            ),
        )
    my_rows = pl.ds(pl.multiple_of(core * own, own), own)
    other_rows = pl.ds(pl.multiple_of((1 - core) * own, own), own)
    second = pl.ds(half, half)
    last_send[1] = held[other_rows, second].astype(BF16)
    lasts = [sent(last_send.at[1], last_recv.at[1], to_core)]
    out_ref[:, pl.ds(pl.multiple_of(core * cols + half, half), half)] = held[
        my_rows, second
    ].astype(BF16)
    turn.wait_recv()
    first = pl.ds(0, half)
    last_send[0] = (held[other_rows, first] + turn_recv[other_rows, :].astype(F32)).astype(BF16)
    lasts.append(sent(last_send.at[0], last_recv.at[0], to_core))
    out_ref[:, pl.ds(pl.multiple_of(core * cols, half), half)] = (
        held[my_rows, first] + turn_recv[my_rows, :].astype(F32)
    ).astype(BF16)
    for s, copy in ((1, lasts[0]), (0, lasts[1])):
        copy.wait_recv()
        out_ref[:, pl.ds(pl.multiple_of((1 - core) * cols + s * half, half), half)] = last_recv[s]
    for copy in used:
        copy.wait_send()


COPIES = 24


def projected(mixed, weight):
    tokens, depth = mixed.shape
    outs = weight.shape[1]
    cols = outs // 2
    half, quarter = cols // 2, cols // 4
    block = tokens // 4
    sub = block // 2
    own = sub // 2
    anywhere = pl.BlockSpec(memory_space=pl.ANY)
    pairs = [
        (4, sub, half),
        (2, block, quarter),
        (2, 2, block, quarter),
        (2, sub, quarter),
        (2, 2, sub, quarter),
        (sub, half),
    ]
    return pl.pallas_call(
        project_kernel,
        out_shape=jax.ShapeDtypeStruct((own, outs), BF16),
        in_specs=[anywhere, anywhere],
        out_specs=pl.BlockSpec(memory_space=pltpu.VMEM),
        scratch_shapes=[
            pltpu.VMEM((tokens, 2 * depth), BF16),
            pltpu.VMEM((2 * depth, cols), BF16),
        ]
        + [pltpu.VMEM(shape, BF16) for shape in pairs for _ in range(2)]
        + [
            pltpu.VMEM((sub, cols), F32),
            pltpu.VMEM((2, own, half), BF16),
            pltpu.VMEM((2, own, half), BF16),
            pltpu.SemaphoreType.DMA((5,)),
            pltpu.SemaphoreType.DMA((COPIES,)),
            pltpu.SemaphoreType.DMA((COPIES,)),
        ],
        compiler_params=pltpu.CompilerParams(
            collective_id=1, has_side_effects=True, vmem_limit_bytes=56 * 2**20
        ),
        name="project",
    )(mixed, weight)


def on_device(featurized, short_filter, decay_rate, residue, skip_gain, out_weight):
    mixed = convolved(featurized, short_filter, decay_rate, residue, skip_gain)
    return projected(mixed, out_weight)


def solution(mesh):
    finer = Mesh(
        mesh.devices.reshape(mesh.shape["ctx"], 4, 2, 2), ("ctx", "chan_0", "chan_1", "chan_2")
    )
    placed = (
        P("ctx", None, CHAN),
        P(None, None, CHAN),
        P(CHAN, None),
        P(CHAN, None),
        P(CHAN),
        P(CHAN, None),
    )
    return jax.shard_map(
        on_device, mesh=finer, in_specs=placed, out_specs=P(CTX_CHAN, None), check_vma=False
    )
```

time: 2370 us -> 116 us (0.05)
  local copies, waits for them, and re-layouts: 2050 us -> 8.11 us
  waiting for transfers between devices: 152 us -> 0 us
  Pallas kernels: 0 us -> 107 us
  matrix products: 82.6 us -> 0 us
  other arithmetic: 56.7 us -> 0.11 us
    gather x16 -> x0, local copies, waits for them, and re-layouts: 1900 us -> none  [own_block(): toeplitz = jnp.take(segment, offsets, axis=1)]
    reduce_scatter x3 -> x0, waiting for transfers between devices: 152 us -> none  [own_block_2(): pieces = lax.psum_scatter(pieces, axes[k], scatter_dimension=0, tiled=True)]
    pallas_call x0 -> x2, Pallas kernels: none -> 107 us  [the longest x1 72.6 us: projected(): pl.pallas_call(project_kernel, out_shape=jax.ShapeDtypeStruct((own, outs)...]
    scatter-add x5 -> x0, local copies, waits for them, and re-layouts: 106 us -> none  [own_block(): summed = summed.at[:, :, lag_tile:].add(product)]
    dot_general x11 -> x0, matrix products: 82.6 us -> none  [the longest x8 60.9 us: own_block(): jnp.einsum('fts,fgps->fgpt', toeplitz, tiles[:, :, :tile_count - lag_tile...]
    add x6 -> x0, other arithmetic: 27.9 us -> none  [the longest x5 16.2 us: own_block(): summed = summed.at[:, :, lag_tile:].add(product)]
  transfers between devices with their start and end apart: 5 -> 0, of which waited for: 3 -> 0; matrix products, arithmetic and copies ran while one was open for 89% -> 0% of each run, Pallas kernels for 0% -> 0%
where the time goes in v1:
time: 116 us
  Pallas kernels  107 us (92%)
  local copies, waits for them, and re-layouts  8.11 us (7%)
    pallas_call x1, Pallas kernels, projected(): pl.pallas_call(project_kernel, out_shape=jax.ShapeDtypeStruct((own, outs)...  72.6 us
    pallas_call x1, Pallas kernels, convolved(): pl.pallas_call(conv_kernel, out_shape=jax.ShapeDtypeStruct((tokens, chann...  34.6 us
    unnamed x7, local copies, waits for them, and re-layouts  5.89 us

profile of v1, /device:TPU:1, one launch (start us, length us, event | category | flops | bytes accessed | tf_op | source)
XLA Modules:
  0.0 115.5 jit_solution(16321650392552984287)
XLA Ops:
  0.0 0.1 pad.7.clone
  0.1 0.8 copy.21
  0.8 0.8 copy.26
  1.7 0.8 tile.10
  2.4 0.1 copy.28
  2.5 0.1 maximum_maximum_fusion.1
  2.6 0.1 copy.29.skip_ref
  2.7 0.1 broadcast_in_dim.9.rate_ref
  2.8 0.1 broadcast_in_dim.20.scale_ref
  2.9 0.8 broadcast_in_dim.21
  3.8 0.2 reshape.9.rate_chan_ref
  3.9 0.0 copy-start.1
  3.9 0.7 copy-done.1
  4.7 34.6 %conv.1.mixed_hbm = bf16[2048,512]{1,0:T(8,128)(2,1)S(1)} custom-call(bf16[3,2048,512]{2,1,0:T(8,128)(2,1)} %bitcast.3, f32[3,3,512]{2,1,0:T(4,128)S(1)} %copy-done.1, f32[32,128]{1,0:T(8,128)S(1)} %get-tuple-element.6.rate_row_ref, f32[32,128]{1,0:T(8,128)S(1)} %get-tuple-element.5.scale_row_ref, f32[32,16,128]{2,1,0:T(8,128)S(1)} %broadcast_in_dim.9.rate_ref, ...), custom_call_target="tpu_custom_call" | custom-call | tf_op jit(solution)/shard_map/conv/pallas_call | solution.py:270
  39.3 0.0 copy-start
  39.3 1.3 %copy-done = bf16[2048,512]{1,0:T(8,128)(2,1)} copy-done((bf16[2048,512]{1,0:T(8,128)(2,1)}, bf16[2048,512]{1,0:T(8,128)(2,1)S(1)}, u32[]{:S(2)}) %copy-start) | copy-done | bytes 2097176
  40.6 72.6 %project.1 = bf16[128,4096]{1,0:T(8,128)(2,1)} custom-call(bf16[2048,512]{1,0:T(8,128)(2,1)} %copy-done, bf16[512,4096]{1,0:T(8,128)(2,1)} %weight_hbm.1), custom_call_target="tpu_custom_call" | custom-call | tf_op jit(solution)/shard_map/project/pallas_call | solution.py:591
  113.2 2.3 %copy.31 = bf16[128,4096]{1,0:T(8,128)(2,1)} copy(bf16[128,4096]{1,0:T(8,128)(2,1)} %project.1) | data formatting | bytes 2097152
  (3 shorter events, 0.0 us)
Async XLA Ops:
  3.9 0.7 copy-start.1
  39.3 1.3 %copy-start = (bf16[2048,512]{1,0:T(8,128)(2,1)}, bf16[2048,512]{1,0:T(8,128)(2,1)S(1)}, u32[]{:S(2)}) copy-start(bf16[2048,512]{1,0:T(8,128)(2,1)S(1)} %conv.1.mixed_hbm) | copy-start | bytes 6291460

commit v2 on v1

v2 whole, which is shorter than its diff:
```python
import jax
import jax.numpy as jnp
from jax import lax
from jax.experimental import pallas as pl
from jax.experimental.pallas import tpu as pltpu
from jax.sharding import Mesh
from jax.sharding import PartitionSpec as P

CHAN = ("chan_0", "chan_1", "chan_2")
CTX_CHAN = ("ctx", "chan_0", "chan_1", "chan_2")
MESH = pl.DeviceIdType.MESH
F32 = jnp.float32
BF16 = jnp.bfloat16
LANES = 128
TILE = 256
COPIES = 24
STEP = 128
GROUP = 16
PACK = LANES // GROUP
MODES = 16
STRIP = 64
RIM = 16


def swapped(parts, lane_group):
    parts = list(parts)
    for bit in (1, 2, 4):
        low = (lane_group & bit) == 0
        for k in range(PACK):
            if k & bit == 0:
                a, b = parts[k], parts[k | bit]
                parts[k] = jnp.where(low, a, pltpu.roll(b, bit * GROUP, 1))
                parts[k | bit] = jnp.where(low, pltpu.roll(a, LANES - bit * GROUP, 1), b)
    return parts


def hi_lo(value):
    hi = value.astype(BF16).astype(F32)
    return hi, value - hi


def one_less_exp(x):
    series = jnp.ones_like(x)
    for n in range(9, 1, -1):
        series = 1.0 - x * (1.0 / n) * series
    return jnp.where(x < 0.5, x * series, 1.0 - jnp.exp(-x))


def chunk_scan(state, rate, lane):
    width = state.shape[1]
    hop = 1
    while hop * GROUP < width:
        decay = jnp.exp(rate * (-float(hop * STEP)))
        moved = pltpu.roll(state, hop * GROUP, 1)
        state = state + jnp.where(lane >= hop * GROUP, decay * moved, 0.0)
        hop *= 2
    return state


def kernel(
    feat_hbm,
    taps_hbm,
    rate_hbm,
    residue_hbm,
    skip_hbm,
    weight_hbm,
    out_ref,
    feat,
    taps,
    rate_in,
    residue_in,
    skip_in,
    skip,
    square,
    rate_row,
    scale_row,
    rates,
    scales,
    rim,
    gated,
    query,
    source,
    left,
    local,
    total,
    totals,
    result,
    mixed,
    weight,
    z_send,
    z_recv,
    far_send,
    far_recv,
    near_send,
    near_recv,
    far2_send,
    far2_recv,
    near2_send,
    near2_recv,
    turn_send,
    turn_recv,
    held,
    last_send,
    last_recv,
    small_sem,
    load_sem,
    rim_sem,
    sum_send,
    sum_recv,
    send_sem,
    recv_sem,
):
    tokens, channels = feat.shape[1], feat.shape[2]
    filters = rates.shape[0]
    chunks = tokens // STEP
    blocks = channels // LANES
    width = chunks * GROUP
    halves = width // LANES
    depth = channels
    cols = weight.shape[1]
    half = cols // 2
    quarter = cols // 4
    block = tokens // 4
    sub = block // 2
    own = sub // 2
    ctx = lax.axis_index("ctx")
    peers = lax.axis_size("ctx")
    x = lax.axis_index("chan_0")
    z = lax.axis_index("chan_1")
    core = lax.axis_index("chan_2")
    right, far, lefts = lax.rem(x + 1, 4), lax.rem(x + 2, 4), lax.rem(x + 3, 4)
    to_right, to_left = {"chan_0": right}, {"chan_0": lefts}
    to_z, to_core = {"chan_1": 1 - z}, {"chan_2": 1 - core}

    smalls = []
    for k, (here, there) in enumerate(
        (
            (rate_hbm, rate_in),
            (residue_hbm, residue_in),
            (taps_hbm, taps),
            (skip_hbm, skip_in),
        )
    ):
        copy = pltpu.make_async_copy(here, there, small_sem.at[k])
        copy.start()
        smalls.append(copy)

    def load_of(v):
        at = pl.ds(pl.multiple_of(v * LANES, LANES), LANES)
        return pltpu.make_async_copy(feat_hbm.at[:, :, at], feat.at[:, :, at], load_sem.at[v])

    for v in range(blocks):
        load_of(v).start()
    my_cols = pl.ds(pl.multiple_of(core * cols, cols), cols)
    other_cols = pl.ds(pl.multiple_of((1 - core) * cols, cols), cols)
    load_weight = pltpu.make_async_copy(
        weight_hbm.at[:, my_cols], weight.at[pl.ds(0, depth), :], load_sem.at[blocks]
    )
    load_weight.start()

    barrier = pltpu.get_barrier_semaphore()
    greeted = [{"ctx": lax.rem(ctx + d, peers)} for d in range(1, peers)]
    greeted += [to_right, to_left, to_z, to_core]
    for to in greeted:
        pl.semaphore_signal(barrier, inc=1, device_id=to, device_id_type=MESH)

    lane = lax.broadcasted_iota(jnp.int32, (1, LANES), 1)
    lane_group = lane // GROUP
    lane_wide = lax.broadcasted_iota(jnp.int32, (MODES, width), 1)
    lane_mode = lax.broadcasted_iota(jnp.int32, (MODES, LANES), 1)
    row = lax.broadcasted_iota(jnp.int32, (STEP, LANES), 0)
    col = lax.broadcasted_iota(jnp.int32, (STEP, LANES), 1)
    after = (row + 1).astype(F32)
    back = lax.rem(STEP - lane_mode, STEP).astype(F32)
    ahead = (STEP - 1 - lane_mode).astype(F32)

    for copy in smalls:
        copy.wait()
    rate_all = rate_in[...]
    scale_all = residue_in[...] * jnp.sqrt(one_less_exp(2.0 * rate_all))
    for f in range(filters):
        rates[f] = jnp.broadcast_to(rate_all[:, f : f + 1], (MODES, LANES))
        scales[f] = jnp.broadcast_to(scale_all[:, f : f + 1], (MODES, LANES))
    square[...] = jnp.zeros_like(square)
    for k in range(3):
        square[k * MODES : (k + 1) * MODES, 0:filters] = rate_all
    rate_row[...] = square[...].T[:filters]
    for k in range(3):
        square[k * MODES : (k + 1) * MODES, 0:filters] = scale_all
    scale_row[...] = square[...].T[:filters]
    skip[...] = skip_in[...].reshape(1, channels)
    source[:, STEP + 3 * MODES :, :] = jnp.zeros(
        (filters, source.shape[1] - STEP - 3 * MODES, width), BF16
    )

    def gate(v, c, earlier_of):
        at = pl.ds(pl.multiple_of(v * LANES, LANES), LANES)
        here = pl.ds(pl.multiple_of(c * STEP, STEP), STEP)
        parts = []
        for i in range(3):
            rows = jnp.concatenate(
                [earlier_of(i, at).astype(F32), feat[i, here, at].astype(F32)], axis=0
            )
            tap = taps[:, i, at]
            value = (
                tap[0:1] * rows[RIM:]
                + tap[1:2] * pltpu.roll(rows, 1, 0)[RIM:]
                + tap[2:3] * pltpu.roll(rows, 2, 0)[RIM:]
            )
            parts.append(value)
        query[here, at] = parts[0].astype(BF16)
        gated[here, at] = (parts[1] * parts[2]).astype(BF16)

    def gate_block(v, carry):
        load_of(v).wait()

        def one_chunk(c, inner):
            before = pl.ds(pl.multiple_of(c * STEP - RIM, RIM), RIM)
            gate(v, c, lambda i, at: feat[i, before, at])
            return inner

        lax.fori_loop(1, chunks, one_chunk, 0)
        return carry

    def gate_first(v, carry):
        gate(v, 0, lambda i, at: jnp.where(ctx > 0, rim[i, :, at].astype(F32), 0.0))
        return carry

    def swap_in(v, h):
        at = pl.ds(pl.multiple_of(v * LANES, LANES), LANES)

        def one_strip(s, inner):
            rows = pl.ds(pl.multiple_of(s * STRIP, STRIP), STRIP)
            parts = []
            for k in range(PACK):
                here = pl.ds(pl.multiple_of((h * PACK + k) * STEP + s * STRIP, STRIP), STRIP)
                parts.append(gated[here, at])
            for g, part in enumerate(swapped(parts, lane_group)):
                source[v * PACK + g, rows, h * LANES : (h + 1) * LANES] = part
            return inner

        lax.fori_loop(0, STEP // STRIP, one_strip, 0)

    lax.fori_loop(0, blocks // 2, gate_block, 0)

    with jax.named_scope("c_barrier"):
        pl.semaphore_wait(barrier, len(greeted))
    rim_copy = pltpu.make_async_remote_copy(
        src_ref=feat_hbm.at[:, pl.ds(tokens - RIM, RIM), :],
        dst_ref=rim,
        send_sem=rim_sem.at[0],
        recv_sem=rim_sem.at[1],
        device_id={"ctx": lax.rem(ctx + 1, peers)},
        device_id_type=MESH,
    )
    rim_copy.start()
    used = []

    def sent(src, dst, to):
        k = len(used)
        copy = pltpu.make_async_remote_copy(
            src_ref=src,
            dst_ref=dst,
            send_sem=send_sem.at[k],
            recv_sem=recv_sem.at[k],
            device_id=to,
            device_id_type=MESH,
        )
        copy.start()
        used.append(copy)
        return copy

    weight_copy = sent(weight_hbm.at[:, other_cols], weight.at[pl.ds(depth, depth), :], to_core)

    lax.fori_loop(blocks // 2, blocks, gate_block, 0)

    def swap_later(v, carry):
        for h in range(1, halves):
            swap_in(v, h)
        return carry

    lax.fori_loop(0, blocks, swap_later, 0)
    with jax.named_scope("c_rim"):
        rim_copy.wait()
    lax.fori_loop(0, blocks, gate_first, 0)

    def state_block(v, carry):
        at = pl.ds(pl.multiple_of(v * LANES, LANES), LANES)
        swap_in(v, 0)
        packed = jnp.zeros((MODES, LANES), F32)
        for g in range(PACK):
            f = v * PACK + g
            rate = rates[f]
            hi, lo = hi_lo(jnp.exp(-rate * ahead))
            factor = jnp.concatenate([hi, lo], axis=0).astype(BF16)
            product = jnp.dot(factor, source[f, :STEP, :], preferred_element_type=F32)
            ends = product[:MODES] + product[MODES:]
            local[f] = ends
            summed = chunk_scan(ends, jnp.concatenate([rate] * halves, axis=1), lane_wide)
            last = summed[:, width - LANES :]
            last = pltpu.roll(last, (g * GROUP + GROUP) % LANES, 1)
            packed = jnp.where(lane_group == g, last, packed)
        total[:, at] = packed
        return carry

    lax.fori_loop(0, blocks, state_block, 0)

    sums = []
    for d in range(1, peers):
        copy = pltpu.make_async_remote_copy(
            src_ref=total,
            dst_ref=totals.at[d - 1],
            send_sem=sum_send.at[d - 1],
            recv_sem=sum_recv.at[d - 1],
            device_id={"ctx": lax.rem(ctx + d, peers)},
            device_id_type=MESH,
        )
        copy.start()
        sums.append(copy)

    def build(f, carry):
        first = jnp.sum(scales[f] * jnp.exp(-rates[f] * back), axis=0, keepdims=True)
        turned = pltpu.roll(
            jnp.broadcast_to(first, (STEP, LANES)), 0, 1, stride=1, stride_axis=0
        )
        left[f, :, :LANES] = jnp.where(col <= row, turned, 0.0).astype(BF16)
        hi, lo = hi_lo(scale_row[pl.ds(f, 1), :] * jnp.exp(-rate_row[pl.ds(f, 1), :] * after))
        second = (col >= MODES) & (col < 2 * MODES)
        left[f, :, LANES:] = jnp.where(second, lo, hi).astype(BF16)
        return carry

    with jax.named_scope("c_build"):
        lax.fori_loop(0, filters, build, 0)
    with jax.named_scope("c_sums"):
        for copy in sums:
            copy.wait()
    for v in range(blocks):
        at = pl.ds(v * LANES, LANES)
        chan_rate = rates[v * PACK]
        for g in range(1, PACK):
            chan_rate = jnp.where(lane_group == g, rates[v * PACK + g], chan_rate)
        carried = jnp.zeros((MODES, LANES), F32)
        for d in range(1, peers):
            decay = jnp.exp(chan_rate * (-float((d - 1) * tokens)))
            carried = carried + jnp.where(ctx >= d, decay * totals[d - 1, :, at], 0.0)
        total[:, at] = carried

    def state_rows(v, carry):
        at = pl.ds(pl.multiple_of(v * LANES, LANES), LANES)
        incoming = total[:, at]
        for g in range(PACK):
            f = v * PACK + g
            entry = pltpu.roll(incoming, (LANES - g * GROUP) % LANES, 1)
            entry = jnp.concatenate([entry] * halves, axis=1)
            states = jnp.where(lane_wide < GROUP, entry, pltpu.roll(local[f], GROUP, 1))
            states = chunk_scan(
                states, jnp.concatenate([rates[f]] * halves, axis=1), lane_wide
            )
            hi, lo = hi_lo(states)
            source[f, STEP : STEP + 3 * MODES, :] = jnp.concatenate([hi, hi, lo], axis=0).astype(
                BF16
            )
        return carry

    with jax.named_scope("c_states"):
        lax.fori_loop(0, blocks, state_rows, 0)

    def block_out(h):
        def one_block(v, carry):
            at = pl.ds(pl.multiple_of(v * LANES, LANES), LANES)
            wide = pl.ds(pl.multiple_of(h * LANES, LANES), LANES)
            for g in range(PACK):
                f = v * PACK + g
                result[g] = jnp.dot(
                    left[f], source[f, :, wide], preferred_element_type=F32
                ).astype(BF16)

            def one_strip(s, inner):
                rows = pl.ds(pl.multiple_of(s * STRIP, STRIP), STRIP)
                parts = swapped([result[g, rows, :] for g in range(PACK)], lane_group)
                for k in range(PACK):
                    here = pl.ds(
                        pl.multiple_of((h * PACK + k) * STEP + s * STRIP, STRIP), STRIP
                    )
                    value = parts[k].astype(F32) + skip[:, at] * gated[here, at].astype(F32)
                    mixed[here, at] = (query[here, at].astype(F32) * value).astype(BF16)
                return inner

            lax.fori_loop(0, STEP // STRIP, one_strip, 0)
            return carry

        return one_block

    def passed_on(at):
        rows = pl.ds(pl.multiple_of(at * block, block), block)
        return sent(
            mixed.at[rows, pl.ds(0, depth)], mixed.at[rows, pl.ds(depth, depth)], to_core
        )

    first_half = far // 2
    with jax.named_scope("c_half1"):
        lax.fori_loop(0, blocks, block_out(first_half), 0)
    passed = [passed_on(far), passed_on(far + 1 - 2 * lax.rem(far, 2))]
    lax.fori_loop(0, 1, block_out(1 - first_half), 0)

    def tiles(token, rows, first, count, store):
        wide = count // TILE

        def one(n, carry):
            i, j = n // wide, lax.rem(n, wide)
            r = pl.multiple_of(i * sub, sub)
            c = pl.multiple_of(j * TILE, TILE)
            value = jnp.dot(
                mixed[pl.ds(pl.multiple_of(token + r, sub), sub), :],
                weight[:, pl.ds(pl.multiple_of(first + c, TILE), TILE)],
                preferred_element_type=F32,
            )
            store(pl.ds(r, sub), pl.ds(c, TILE), value)
            return carry

        lax.fori_loop(0, (rows // sub) * wide, one, 0)

    def start_of(at):
        return at * block

    def plain(dst, extra=()):
        def store(r, c, value):
            for e in extra:
                value = value + e[r, c].astype(F32)
            dst[r, c] = value.astype(BF16)

        return store

    mine, others = z * sub, (1 - z) * sub
    order = (far, right, lefts, x)

    def z_first(k):
        at = order[k]
        tiles(start_of(at) + others, sub, half, half, plain(z_send.at[k]))
        return sent(z_send.at[k], z_recv.at[k], to_z)

    with jax.named_scope("c_w_start"):
        load_weight.wait()
        weight_copy.wait_recv()
        passed[0].wait_recv()
    zs = [z_first(0)]
    fars = []
    for s, to in ((0, to_right), (1, to_left)):
        tiles(start_of(far), block, s * quarter, quarter, plain(far_send.at[s]))
        fars.append(sent(far_send.at[s], far_recv.at[s], to))

    with jax.named_scope("c_half2"):
        lax.fori_loop(1, blocks, block_out(1 - first_half), 0)
    passed += [passed_on(x + 1 - 2 * lax.rem(x, 2)), passed_on(x)]
    with jax.named_scope("c_w_passed"):
        for copy in passed[1:]:
            copy.wait_recv()
    zs.append(z_first(1))
    sides = ((0, right, to_right), (1, lefts, to_left))
    nears = {}
    for s, at, to in sides:
        side = 1 - s
        tiles(start_of(at), block, side * quarter, quarter, plain(near_send.at[s, side]))
        nears[s, side] = sent(near_send.at[s, side], near_recv.at[s, side], to)
    zs.append(z_first(2))
    zs.append(z_first(3))

    with jax.named_scope("c_w_z0"):
        zs[0].wait_recv()
    fars2 = []
    for s, to in ((0, to_right), (1, to_left)):
        at = pl.ds(s * quarter, quarter)
        tiles(
            start_of(far) + mine,
            sub,
            half + s * quarter,
            quarter,
            plain(far2_send.at[s], (z_recv.at[0, :, at],)),
        )
        fars2.append(sent(far2_send.at[s], far2_recv.at[s], to))
    for s, at, to in sides:
        with jax.named_scope("c_w_far"):
            fars[s].wait_recv()
        tiles(
            start_of(at), block, s * quarter, quarter, plain(near_send.at[s, s], (far_recv.at[s],))
        )
        nears[s, s] = sent(near_send.at[s, s], near_recv.at[s, s], to)

    nears2 = {}
    for s, at, to in sides:
        with jax.named_scope("c_w_z12"):
            zs[1 + s].wait_recv()
        side = 1 - s
        piece = pl.ds(side * quarter, quarter)
        tiles(
            start_of(at) + mine,
            sub,
            half + side * quarter,
            quarter,
            plain(near2_send.at[s, side], (z_recv.at[1 + s, :, piece],)),
        )
        nears2[s, side] = sent(near2_send.at[s, side], near2_recv.at[s, side], to)
    for s, at, to in sides:
        with jax.named_scope("c_w_far2"):
            fars2[s].wait_recv()
        piece = pl.ds(s * quarter, quarter)
        tiles(
            start_of(at) + mine,
            sub,
            half + s * quarter,
            quarter,
            plain(near2_send.at[s, s], (z_recv.at[1 + s, :, piece], far2_recv.at[s])),
        )
        nears2[s, s] = sent(near2_send.at[s, s], near2_recv.at[s, s], to)

    with jax.named_scope("c_w_near"):
        for copy in nears.values():
            copy.wait_recv()
    for side in (0, 1):
        piece = pl.ds(side * quarter, quarter)
        away = pl.ds(pl.multiple_of(others, sub), sub)
        tiles(
            start_of(x) + others,
            sub,
            side * quarter,
            quarter,
            plain(
                turn_send.at[:, piece],
                (near_recv.at[0, side, away], near_recv.at[1, side, away]),
            ),
        )
    turn = sent(turn_send, turn_recv, to_z)

    def kept(offset, extra):
        def store(r, c, value):
            for e in extra:
                value = value + e[r, c].astype(F32)
            held[r, pl.ds(pl.multiple_of(offset + c.start, TILE), TILE)] = value

        return store

    for side in (0, 1):
        here = pl.ds(pl.multiple_of(mine, sub), sub)
        tiles(
            start_of(x) + mine,
            sub,
            side * quarter,
            quarter,
            kept(side * quarter, (near_recv.at[0, side, here], near_recv.at[1, side, here])),
        )
    with jax.named_scope("c_w_z3"):
        zs[3].wait_recv()
    for side in (0, 1):
        piece = pl.ds(side * quarter, quarter)
        tiles(
            start_of(x) + mine,
            sub,
            half + side * quarter,
            quarter,
            kept(half + side * quarter, (z_recv.at[3, :, piece],)),
        )
    my_rows = pl.ds(pl.multiple_of(core * own, own), own)
    other_rows = pl.ds(pl.multiple_of((1 - core) * own, own), own)
    my_first = pl.multiple_of(core * cols, cols)
    with jax.named_scope("c_w_near2"):
        for copy in nears2.values():
            copy.wait_recv()
    for rows, keep in ((other_rows, False), (my_rows, True)):
        for side in (0, 1):
            at = pl.ds(half + side * quarter, quarter)
            value = (
                held[rows, at]
                + near2_recv[0, side, rows, :].astype(F32)
                + near2_recv[1, side, rows, :].astype(F32)
            ).astype(BF16)
            if keep:
                out_ref[:, pl.ds(my_first + half + side * quarter, quarter)] = value
            else:
                last_send[1, :, side * quarter : (side + 1) * quarter] = value
        if not keep:
            lasts = [sent(last_send.at[1], last_recv.at[1], to_core)]
    with jax.named_scope("c_w_turn"):
        turn.wait_recv()
    first = pl.ds(0, half)
    last_send[0] = (held[other_rows, first] + turn_recv[other_rows, :].astype(F32)).astype(BF16)
    lasts.append(sent(last_send.at[0], last_recv.at[0], to_core))
    out_ref[:, pl.ds(my_first, half)] = (
        held[my_rows, first] + turn_recv[my_rows, :].astype(F32)
    ).astype(BF16)
    for s, copy in ((1, lasts[0]), (0, lasts[1])):
        with jax.named_scope("c_w_last"):
            copy.wait_recv()
        out_ref[:, pl.ds(pl.multiple_of((1 - core) * cols + s * half, half), half)] = last_recv[s]
    for copy in used:
        copy.wait_send()


def on_device(featurized, short_filter, decay_rate, residue, skip_gain, weight):
    tokens, _, channels = featurized.shape
    filters = decay_rate.shape[0]
    peers = lax.axis_size("ctx")
    chunks = tokens // STEP
    width = chunks * GROUP
    outs = weight.shape[1]
    cols = outs // 2
    half, quarter = cols // 2, cols // 4
    block = tokens // 4
    sub = block // 2
    own = sub // 2
    pairs = [
        (4, sub, half),
        (2, block, quarter),
        (2, 2, block, quarter),
        (2, sub, quarter),
        (2, 2, sub, quarter),
        (sub, half),
    ]
    return pl.pallas_call(
        kernel,
        out_shape=jax.ShapeDtypeStruct((own, outs), BF16),
        in_specs=[pl.BlockSpec(memory_space=pl.ANY)] * 6,
        out_specs=pl.BlockSpec(memory_space=pltpu.VMEM),
        scratch_shapes=[
            pltpu.VMEM((3, tokens, channels), BF16),
            pltpu.VMEM(short_filter.shape, F32),
            pltpu.VMEM((MODES, filters), F32),
            pltpu.VMEM((MODES, filters), F32),
            pltpu.VMEM((channels,), F32),
            pltpu.VMEM((1, channels), F32),
            pltpu.VMEM((LANES, LANES), F32),
            pltpu.VMEM((filters, LANES), F32),
            pltpu.VMEM((filters, LANES), F32),
            pltpu.VMEM((filters, MODES, LANES), F32),
            pltpu.VMEM((filters, MODES, LANES), F32),
            pltpu.VMEM((3, RIM, channels), BF16),
            pltpu.VMEM((tokens, channels), BF16),
            pltpu.VMEM((tokens, channels), BF16),
            pltpu.VMEM((filters, 2 * STEP, width), BF16),
            pltpu.VMEM((filters, STEP, 2 * LANES), BF16),
            pltpu.VMEM((filters, MODES, width), F32),
            pltpu.VMEM((MODES, channels), F32),
            pltpu.VMEM((peers - 1, MODES, channels), F32),
            pltpu.VMEM((PACK, STEP, LANES), BF16),
            pltpu.VMEM((tokens, 2 * channels), BF16),
            pltpu.VMEM((2 * channels, cols), BF16),
        ]
        + [pltpu.VMEM(shape, BF16) for shape in pairs for _ in range(2)]
        + [
            pltpu.VMEM((sub, cols), F32),
            pltpu.VMEM((2, own, half), BF16),
            pltpu.VMEM((2, own, half), BF16),
            pltpu.SemaphoreType.DMA((4,)),
            pltpu.SemaphoreType.DMA((channels // LANES + 1,)),
            pltpu.SemaphoreType.DMA((2,)),
            pltpu.SemaphoreType.DMA((peers - 1,)),
            pltpu.SemaphoreType.DMA((peers - 1,)),
            pltpu.SemaphoreType.DMA((COPIES,)),
            pltpu.SemaphoreType.DMA((COPIES,)),
        ],
        compiler_params=pltpu.CompilerParams(
            collective_id=0, has_side_effects=True, vmem_limit_bytes=60 * 2**20
        ),
        name="hyena",
    )(
        featurized.transpose(1, 0, 2),
        short_filter,
        decay_rate.T,
        residue.T,
        skip_gain,
        weight,
    )


def solution(mesh):
    finer = Mesh(
        mesh.devices.reshape(mesh.shape["ctx"], 4, 2, 2), ("ctx", "chan_0", "chan_1", "chan_2")
    )
    placed = (
        P("ctx", None, CHAN),
        P(None, None, CHAN),
        P(CHAN, None),
        P(CHAN, None),
        P(CHAN),
        P(CHAN, None),
    )
    return jax.shard_map(
        on_device, mesh=finer, in_specs=placed, out_specs=P(CTX_CHAN, None), check_vma=False
    )
```

time: 116 us -> 97.8 us (0.84)
  Pallas kernels: 107 us -> 95.3 us
  local copies, waits for them, and re-layouts: 8.11 us -> 2.29 us
    pallas_call x2 -> x1, Pallas kernels: 107 us -> 95.3 us  [on_device(): pl.pallas_call(kernel, out_shape=jax.ShapeDtypeStruct((own, outs), BF16),...]
    unnamed x7 -> x1, local copies, waits for them, and re-layouts: 5.89 us -> 2.29 us
where the time goes in v2:
time: 97.8 us; the launch traced here: 97.6 us
  Pallas kernels  95.3 us (97%)
  local copies, waits for them, and re-layouts  2.29 us (2%)
    pallas_call x1, Pallas kernels, on_device(): pl.pallas_call(kernel, out_shape=jax.ShapeDtypeStruct((own, outs), BF16),...  95.3 us
    unnamed x1, local copies, waits for them, and re-layouts  2.29 us

profile of v2, /device:TPU:1, one launch (start us, length us, event | category | flops | bytes accessed | tf_op | source)
XLA Modules:
  0.0 97.6 jit_solution(5661488752891607510)
XLA Ops:
  0.0 95.3 %hyena.1 = bf16[128,4096]{1,0:T(8,128)(2,1)} custom-call(bf16[3,2048,512]{2,1,0:T(8,128)(2,1)} %bitcast.3, f32[3,3,512]{2,1,0:T(4,128)} %taps_hbm.1, f32[16,32]{1,0:T(8,128)} %bitcast.4, f32[16,32]{1,0:T(8,128)} %bitcast.5, f32[512]{0:T(512)} %skip_hbm.1, bf16[512,4096]{1,0:T(8,128)(2,1)} %weight_hbm.1), custom_call_target="tpu_custom_call" | custom-call | tf_op jit(solution)/shard_map/hyena/pallas_call | solution.py:618
  95.3 2.3 %copy.8 = bf16[128,4096]{1,0:T(8,128)(2,1)} copy(bf16[128,4096]{1,0:T(8,128)(2,1)} %hyena.1) | data formatting | bytes 2097152

commit v3 on v2

--- a/solution.py
+++ b/solution.py
@@ -13,7 +13,7 @@
 BF16 = jnp.bfloat16
 LANES = 128
 TILE = 256
-COPIES = 24
+COPIES = 25
 STEP = 128
 GROUP = 16
 PACK = LANES // GROUP
@@ -22,16 +22,24 @@
 RIM = 16
 
 
-def swapped(parts, lane_group):
-    parts = list(parts)
+def turned_to(parts, lane_group, sign):
     for bit in (1, 2, 4):
-        low = (lane_group & bit) == 0
-        for k in range(PACK):
-            if k & bit == 0:
-                a, b = parts[k], parts[k | bit]
-                parts[k] = jnp.where(low, a, pltpu.roll(b, bit * GROUP, 1))
-                parts[k | bit] = jnp.where(low, pltpu.roll(a, LANES - bit * GROUP, 1), b)
+        move = (lane_group & bit) != 0
+        parts = [
+            jnp.where(move, parts[(k + sign * bit) % PACK], parts[k]) for k in range(PACK)
+        ]
     return parts
+
+
+def by_filter(parts, lane_group):
+    parts = [pltpu.roll(part, k * GROUP, 1) if k else part for k, part in enumerate(parts)]
+    parts = turned_to(parts, lane_group, 1)
+    return [parts[-g % PACK] for g in range(PACK)]
+
+
+def by_chunk(parts, lane_group):
+    parts = turned_to([parts[-k % PACK] for k in range(PACK)], lane_group, -1)
+    return [pltpu.roll(part, LANES - k * GROUP, 1) if k else part for k, part in enumerate(parts)]
 
 
 def hi_lo(value):
@@ -46,15 +54,16 @@
     return jnp.where(x < 0.5, x * series, 1.0 - jnp.exp(-x))
 
 
-def chunk_scan(state, rate, lane):
-    width = state.shape[1]
-    hop = 1
-    while hop * GROUP < width:
+def chunk_scan(low, high, rate, place):
+    for hop in (1, 2, 4):
         decay = jnp.exp(rate * (-float(hop * STEP)))
-        moved = pltpu.roll(state, hop * GROUP, 1)
-        state = state + jnp.where(lane >= hop * GROUP, decay * moved, 0.0)
-        hop *= 2
-    return state
+        inside = place >= hop
+        a, b = pltpu.roll(low, hop * GROUP, 1), pltpu.roll(high, hop * GROUP, 1)
+        low, high = (
+            low + decay * jnp.where(inside, a, 0.0),
+            high + decay * jnp.where(inside, b, a),
+        )
+    return low, high + jnp.exp(rate * (-float(PACK * STEP))) * low
 
 
 def kernel(
@@ -82,6 +91,8 @@
     source,
     left,
     local,
+    chan_rates,
+    amend,
     total,
     totals,
     result,
@@ -131,6 +142,7 @@
     right, far, lefts = lax.rem(x + 1, 4), lax.rem(x + 2, 4), lax.rem(x + 3, 4)
     to_right, to_left = {"chan_0": right}, {"chan_0": lefts}
     to_z, to_core = {"chan_1": 1 - z}, {"chan_2": 1 - core}
+    to_both = {"chan_1": 1 - z, "chan_2": 1 - core}
 
     smalls = []
     for k, (here, there) in enumerate(
@@ -160,13 +172,12 @@
 
     barrier = pltpu.get_barrier_semaphore()
     greeted = [{"ctx": lax.rem(ctx + d, peers)} for d in range(1, peers)]
-    greeted += [to_right, to_left, to_z, to_core]
+    greeted += [to_right, to_left, to_z, to_core, to_both]
     for to in greeted:
         pl.semaphore_signal(barrier, inc=1, device_id=to, device_id_type=MESH)
 
     lane = lax.broadcasted_iota(jnp.int32, (1, LANES), 1)
     lane_group = lane // GROUP
-    lane_wide = lax.broadcasted_iota(jnp.int32, (MODES, width), 1)
     lane_mode = lax.broadcasted_iota(jnp.int32, (MODES, LANES), 1)
     row = lax.broadcasted_iota(jnp.int32, (STEP, LANES), 0)
     col = lax.broadcasted_iota(jnp.int32, (STEP, LANES), 1)
@@ -219,14 +230,11 @@
             gate(v, c, lambda i, at: feat[i, before, at])
             return inner
 
+        gate(v, 0, lambda i, at: jnp.zeros((RIM, LANES), F32))
         lax.fori_loop(1, chunks, one_chunk, 0)
         return carry
 
-    def gate_first(v, carry):
-        gate(v, 0, lambda i, at: jnp.where(ctx > 0, rim[i, :, at].astype(F32), 0.0))
-        return carry
-
-    def swap_in(v, h):
+    def swap_in(v, h, strips=STEP // STRIP):
         at = pl.ds(pl.multiple_of(v * LANES, LANES), LANES)
 
         def one_strip(s, inner):
@@ -235,11 +243,11 @@
             for k in range(PACK):
                 here = pl.ds(pl.multiple_of((h * PACK + k) * STEP + s * STRIP, STRIP), STRIP)
                 parts.append(gated[here, at])
-            for g, part in enumerate(swapped(parts, lane_group)):
+            for g, part in enumerate(by_filter(parts, lane_group)):
                 source[v * PACK + g, rows, h * LANES : (h + 1) * LANES] = part
             return inner
 
-        lax.fori_loop(0, STEP // STRIP, one_strip, 0)
+        lax.fori_loop(0, strips, one_strip, 0)
 
     lax.fori_loop(0, blocks // 2, gate_block, 0)
 
@@ -274,19 +282,10 @@
 
     lax.fori_loop(blocks // 2, blocks, gate_block, 0)
 
-    def swap_later(v, carry):
-        for h in range(1, halves):
-            swap_in(v, h)
-        return carry
-
-    lax.fori_loop(0, blocks, swap_later, 0)
-    with jax.named_scope("c_rim"):
-        rim_copy.wait()
-    lax.fori_loop(0, blocks, gate_first, 0)
-
     def state_block(v, carry):
         at = pl.ds(pl.multiple_of(v * LANES, LANES), LANES)
-        swap_in(v, 0)
+        for h in range(halves):
+            swap_in(v, h)
         packed = jnp.zeros((MODES, LANES), F32)
         for g in range(PACK):
             f = v * PACK + g
@@ -296,14 +295,55 @@
             product = jnp.dot(factor, source[f, :STEP, :], preferred_element_type=F32)
             ends = product[:MODES] + product[MODES:]
             local[f] = ends
-            summed = chunk_scan(ends, jnp.concatenate([rate] * halves, axis=1), lane_wide)
-            last = summed[:, width - LANES :]
-            last = pltpu.roll(last, (g * GROUP + GROUP) % LANES, 1)
+            place = (lane_group - g) & (PACK - 1)
+            decay = jnp.exp(-rate * ((PACK - 1 - place) * STEP).astype(F32))
+            whole = jnp.exp(rate * (-float(PACK * STEP)))
+            last = decay * (whole * ends[:, :LANES] + ends[:, LANES:])
+            for hop in (1, 2, 4):
+                last = last + pltpu.roll(last, hop * GROUP, 1)
             packed = jnp.where(lane_group == g, last, packed)
         total[:, at] = packed
         return carry
 
-    lax.fori_loop(0, blocks, state_block, 0)
+    with jax.named_scope("c_state"):
+        lax.fori_loop(0, blocks, state_block, 0)
+
+    def amend_block(v, carry):
+        at = pl.ds(pl.multiple_of(v * LANES, LANES), LANES)
+        parts = []
+        for i in range(3):
+            rows = jnp.concatenate([rim[i, :, at], feat[i, :RIM, at]], axis=0).astype(F32)
+            tap = taps[:, i, at]
+            value = (
+                tap[0:1] * rows[RIM:]
+                + tap[1:2] * pltpu.roll(rows, 1, 0)[RIM:]
+                + tap[2:3] * pltpu.roll(rows, 2, 0)[RIM:]
+            )
+            parts.append(value)
+        new = (lax.broadcasted_iota(jnp.int32, (RIM, LANES), 0) < 2) & (ctx > 0)
+        was = gated[:RIM, at].astype(F32)
+        now = jnp.where(new, (parts[1] * parts[2]).astype(BF16).astype(F32), was)
+        gated[:RIM, at] = now.astype(BF16)
+        query[:RIM, at] = jnp.where(new, parts[0], query[:RIM, at].astype(F32)).astype(BF16)
+        change = now - was
+        rate = rates[v * PACK]
+        for g in range(1, PACK):
+            rate = jnp.where(lane_group == g, rates[v * PACK + g], rate)
+        chan_rates[:, at] = rate
+
+        def effect(count):
+            return (
+                jnp.exp(rate * (-float(count - 1))) * change[0:1]
+                + jnp.exp(rate * (-float(count - 2))) * change[1:2]
+            )
+
+        total[:, at] = total[:, at] + effect(tokens)
+        amend[:, at] = effect(STEP)
+        return carry
+
+    with jax.named_scope("c_rim"):
+        rim_copy.wait()
+    lax.fori_loop(0, blocks, amend_block, 0)
 
     sums = []
     for d in range(1, peers):
@@ -329,6 +369,11 @@
         left[f, :, LANES:] = jnp.where(second, lo, hi).astype(BF16)
         return carry
 
+    def swap_again(v, carry):
+        swap_in(v, 0, 1)
+        return carry
+
+    lax.fori_loop(0, blocks, swap_again, 0)
     with jax.named_scope("c_build"):
         lax.fori_loop(0, filters, build, 0)
     with jax.named_scope("c_sums"):
@@ -336,9 +381,7 @@
             copy.wait()
     for v in range(blocks):
         at = pl.ds(v * LANES, LANES)
-        chan_rate = rates[v * PACK]
-        for g in range(1, PACK):
-            chan_rate = jnp.where(lane_group == g, rates[v * PACK + g], chan_rate)
+        chan_rate = chan_rates[:, at]
         carried = jnp.zeros((MODES, LANES), F32)
         for d in range(1, peers):
             decay = jnp.exp(chan_rate * (-float((d - 1) * tokens)))
@@ -348,14 +391,15 @@
     def state_rows(v, carry):
         at = pl.ds(pl.multiple_of(v * LANES, LANES), LANES)
         incoming = total[:, at]
+        amended = pltpu.roll(amend[:, at], GROUP, 1)
         for g in range(PACK):
             f = v * PACK + g
-            entry = pltpu.roll(incoming, (LANES - g * GROUP) % LANES, 1)
-            entry = jnp.concatenate([entry] * halves, axis=1)
-            states = jnp.where(lane_wide < GROUP, entry, pltpu.roll(local[f], GROUP, 1))
-            states = chunk_scan(
-                states, jnp.concatenate([rates[f]] * halves, axis=1), lane_wide
-            )
+            place = (lane_group - g) & (PACK - 1)
+            a = pltpu.roll(local[f, :, :LANES], GROUP, 1)
+            b = pltpu.roll(local[f, :, LANES:], GROUP, 1)
+            low = jnp.where(place == 0, incoming, a + jnp.where(place == 1, amended, 0.0))
+            high = jnp.where(place == 0, a, b)
+            states = jnp.concatenate(chunk_scan(low, high, rates[f], place), axis=1)
             hi, lo = hi_lo(states)
             source[f, STEP : STEP + 3 * MODES, :] = jnp.concatenate([hi, hi, lo], axis=0).astype(
                 BF16
@@ -377,7 +421,7 @@
 
             def one_strip(s, inner):
                 rows = pl.ds(pl.multiple_of(s * STRIP, STRIP), STRIP)
-                parts = swapped([result[g, rows, :] for g in range(PACK)], lane_group)
+                parts = by_chunk([result[g, rows, :] for g in range(PACK)], lane_group)
                 for k in range(PACK):
                     here = pl.ds(
                         pl.multiple_of((h * PACK + k) * STEP + s * STRIP, STRIP), STRIP
@@ -529,7 +573,12 @@
                 (near_recv.at[0, side, away], near_recv.at[1, side, away]),
             ),
         )
-    turn = sent(turn_send, turn_recv, to_z)
+    my_rows = pl.ds(pl.multiple_of(core * own, own), own)
+    other_rows = pl.ds(pl.multiple_of((1 - core) * own, own), own)
+    turns = [
+        sent(turn_send.at[other_rows], turn_recv.at[1], to_both),
+        sent(turn_send.at[my_rows], turn_recv.at[0], to_z),
+    ]
 
     def kept(offset, extra):
         def store(r, c, value):
@@ -548,6 +597,9 @@
             quarter,
             kept(side * quarter, (near_recv.at[0, side, here], near_recv.at[1, side, here])),
         )
+    first = pl.ds(0, half)
+    last_send[0] = held[other_rows, first].astype(BF16)
+    lasts = [sent(last_send.at[0], last_recv.at[0], to_core)]
     with jax.named_scope("c_w_z3"):
         zs[3].wait_recv()
     for side in (0, 1):
@@ -559,8 +611,6 @@
             quarter,
             kept(half + side * quarter, (z_recv.at[3, :, piece],)),
         )
-    my_rows = pl.ds(pl.multiple_of(core * own, own), own)
-    other_rows = pl.ds(pl.multiple_of((1 - core) * own, own), own)
     my_first = pl.multiple_of(core * cols, cols)
     with jax.named_scope("c_w_near2"):
         for copy in nears2.values():
@@ -578,19 +628,21 @@
             else:
                 last_send[1, :, side * quarter : (side + 1) * quarter] = value
         if not keep:
-            lasts = [sent(last_send.at[1], last_recv.at[1], to_core)]
+            lasts.append(sent(last_send.at[1], last_recv.at[1], to_core))
+    other_first = pl.multiple_of((1 - core) * cols, cols)
+    with jax.named_scope("c_w_last"):
+        lasts[1].wait_recv()
+    out_ref[:, pl.ds(other_first + half, half)] = last_recv[1]
     with jax.named_scope("c_w_turn"):
-        turn.wait_recv()
-    first = pl.ds(0, half)
-    last_send[0] = (held[other_rows, first] + turn_recv[other_rows, :].astype(F32)).astype(BF16)
-    lasts.append(sent(last_send.at[0], last_recv.at[0], to_core))
+        lasts[0].wait_recv()
+        turns[0].wait_recv()
+    out_ref[:, pl.ds(other_first, half)] = (
+        last_recv[0].astype(F32) + turn_recv[1].astype(F32)
+    ).astype(BF16)
+    turns[1].wait_recv()
     out_ref[:, pl.ds(my_first, half)] = (
-        held[my_rows, first] + turn_recv[my_rows, :].astype(F32)
+        held[my_rows, first] + turn_recv[0].astype(F32)
     ).astype(BF16)
-    for s, copy in ((1, lasts[0]), (0, lasts[1])):
-        with jax.named_scope("c_w_last"):
-            copy.wait_recv()
-        out_ref[:, pl.ds(pl.multiple_of((1 - core) * cols + s * half, half), half)] = last_recv[s]
     for copy in used:
         copy.wait_send()
 
@@ -613,12 +665,11 @@
         (2, 2, block, quarter),
         (2, sub, quarter),
         (2, 2, sub, quarter),
-        (sub, half),
     ]
     return pl.pallas_call(
         kernel,
         out_shape=jax.ShapeDtypeStruct((own, outs), BF16),
-        in_specs=[pl.BlockSpec(memory_space=pl.ANY)] * 6,
+        in_specs=[pl.BlockSpec(memory_space=pltpu.HBM)] * 6,
         out_specs=pl.BlockSpec(memory_space=pltpu.VMEM),
         scratch_shapes=[
             pltpu.VMEM((3, tokens, channels), BF16),
@@ -639,6 +690,8 @@
             pltpu.VMEM((filters, STEP, 2 * LANES), BF16),
             pltpu.VMEM((filters, MODES, width), F32),
             pltpu.VMEM((MODES, channels), F32),
+            pltpu.VMEM((MODES, channels), F32),
+            pltpu.VMEM((MODES, channels), F32),
             pltpu.VMEM((peers - 1, MODES, channels), F32),
             pltpu.VMEM((PACK, STEP, LANES), BF16),
             pltpu.VMEM((tokens, 2 * channels), BF16),
@@ -646,6 +699,8 @@
         ]
         + [pltpu.VMEM(shape, BF16) for shape in pairs for _ in range(2)]
         + [
+            pltpu.VMEM((sub, half), BF16),
+            pltpu.VMEM((2, own, half), BF16),
             pltpu.VMEM((sub, cols), F32),
             pltpu.VMEM((2, own, half), BF16),
             pltpu.VMEM((2, own, half), BF16),
@@ -658,16 +713,21 @@
             pltpu.SemaphoreType.DMA((COPIES,)),
         ],
         compiler_params=pltpu.CompilerParams(
-            collective_id=0, has_side_effects=True, vmem_limit_bytes=60 * 2**20
+            collective_id=0, has_side_effects=True, vmem_limit_bytes=50 * 2**20
         ),
         name="hyena",
     )(
-        featurized.transpose(1, 0, 2),
-        short_filter,
-        decay_rate.T,
-        residue.T,
-        skip_gain,
-        weight,
+        *(
+            pltpu.with_memory_space_constraint(array, pltpu.HBM)
+            for array in (
+                featurized.transpose(1, 0, 2),
+                short_filter,
+                decay_rate.T,
+                residue.T,
+                skip_gain,
+                weight,
+            )
+        )
     )
 
 

time: 97.8 us -> 88.9 us (0.909)
  Pallas kernels: 95.3 us -> 87.8 us
  local copies, waits for them, and re-layouts: 2.29 us -> 0.97 us
    pallas_call x1, Pallas kernels: 95.3 us -> 87.8 us  [on_device(): pl.pallas_call(kernel, out_shape=jax.ShapeDtypeStruct((own, outs), BF16),...]
    unnamed x1, local copies, waits for them, and re-layouts: 2.29 us -> 0.97 us
where the time goes in v3:
time: 88.9 us; the launch traced here: 88.8 us
  Pallas kernels  87.8 us (99%)
  local copies, waits for them, and re-layouts  0.97 us (1%)
    pallas_call x1, Pallas kernels, on_device(): pl.pallas_call(kernel, out_shape=jax.ShapeDtypeStruct((own, outs), BF16),...  87.8 us

profile of v3, /device:TPU:1, one launch (start us, length us, event | category | flops | bytes accessed | tf_op | source)
XLA Modules:
  0.0 88.8 jit_solution(7462011352197950824)
XLA Ops:
  0.0 87.8 %hyena.1 = bf16[128,4096]{1,0:T(8,128)(2,1)S(1)} custom-call(bf16[3,2048,512]{2,1,0:T(8,128)(2,1)} %bitcast.3, f32[3,3,512]{2,1,0:T(4,128)} %taps_hbm.1, f32[16,32]{1,0:T(8,128)} %bitcast.4, f32[16,32]{1,0:T(8,128)} %bitcast.5, f32[512]{0:T(512)} %skip_hbm.1, bf16[512,4096]{1,0:T(8,128)(2,1)} %weight_hbm.1), custom_call_target="tpu_custom_call" | custom-call | tf_op jit(solution)/shard_map/hyena/pallas_call | solution.py:669
  87.8 1.0 %copy.8 = bf16[128,4096]{1,0:T(8,128)(2,1)} copy(bf16[128,4096]{1,0:T(8,128)(2,1)S(1)} %hyena.1) | data formatting | bytes 2097152

commit v4 on v3

--- a/solution.py
+++ b/solution.py
@@ -13,7 +13,7 @@
 BF16 = jnp.bfloat16
 LANES = 128
 TILE = 256
-COPIES = 25
+COPIES = 31
 STEP = 128
 GROUP = 16
 PACK = LANES // GROUP
@@ -64,6 +64,15 @@
             high + decay * jnp.where(inside, b, a),
         )
     return low, high + jnp.exp(rate * (-float(PACK * STEP))) * low
+
+
+def column_parts(cols):
+    half = cols * 9 // 16
+    split = cols * 5 // 16
+    later = cols * 3 // 16
+    x_parts = ((0, split), (split, half - split))
+    z_parts = ((0, later), (later, cols - half - later))
+    return half, x_parts, z_parts
 
 
 def kernel(
@@ -86,6 +95,7 @@
     rates,
     scales,
     rim,
+    shifts,
     gated,
     query,
     source,
@@ -111,8 +121,12 @@
     turn_send,
     turn_recv,
     held,
-    last_send,
-    last_recv,
+    last_x_send,
+    last_x_recv,
+    last_z_send,
+    last_z_recv,
+    pass_send,
+    pass_recv,
     small_sem,
     load_sem,
     rim_sem,
@@ -129,8 +143,8 @@
     halves = width // LANES
     depth = channels
     cols = weight.shape[1]
-    half = cols // 2
-    quarter = cols // 4
+    half, x_parts, z_parts = column_parts(cols)
+    rest = cols - half
     block = tokens // 4
     sub = block // 2
     own = sub // 2
@@ -147,9 +161,9 @@
     smalls = []
     for k, (here, there) in enumerate(
         (
+            (taps_hbm, taps),
             (rate_hbm, rate_in),
             (residue_hbm, residue_in),
-            (taps_hbm, taps),
             (skip_hbm, skip_in),
         )
     ):
@@ -161,14 +175,13 @@
         at = pl.ds(pl.multiple_of(v * LANES, LANES), LANES)
         return pltpu.make_async_copy(feat_hbm.at[:, :, at], feat.at[:, :, at], load_sem.at[v])
 
-    for v in range(blocks):
+    for v in range(2):
         load_of(v).start()
     my_cols = pl.ds(pl.multiple_of(core * cols, cols), cols)
     other_cols = pl.ds(pl.multiple_of((1 - core) * cols, cols), cols)
     load_weight = pltpu.make_async_copy(
         weight_hbm.at[:, my_cols], weight.at[pl.ds(0, depth), :], load_sem.at[blocks]
     )
-    load_weight.start()
 
     barrier = pltpu.get_barrier_semaphore()
     greeted = [{"ctx": lax.rem(ctx + d, peers)} for d in range(1, peers)]
@@ -185,8 +198,64 @@
     back = lax.rem(STEP - lane_mode, STEP).astype(F32)
     ahead = (STEP - 1 - lane_mode).astype(F32)
 
-    for copy in smalls:
-        copy.wait()
+    def gate(v, c, slot):
+        at = pl.ds(pl.multiple_of(v * LANES, LANES), LANES)
+        here = pl.ds(pl.multiple_of(c * STEP, STEP), STEP)
+        before = pl.ds(pl.multiple_of(jnp.maximum(c * STEP - RIM, 0), RIM), RIM)
+        parts = []
+        for i in range(3):
+            earlier = feat[i, before, at].astype(F32)
+            now = feat[i, here, at].astype(F32)
+            shifts[slot, i, :RIM] = jnp.where(c > 0, earlier, 0.0)
+            shifts[slot, i, RIM:] = now
+            tap = taps[:, i, at]
+            value = (
+                tap[0:1] * now
+                + tap[1:2] * shifts[slot, i, RIM - 1 : RIM - 1 + STEP]
+                + tap[2:3] * shifts[slot, i, RIM - 2 : RIM - 2 + STEP]
+            )
+            parts.append(value)
+        query[here, at] = parts[0].astype(BF16)
+        gated[here, at] = (parts[1] * parts[2]).astype(BF16)
+
+    def gate_block(v, carry):
+        load_of(v).wait()
+
+        @pl.when(v + 2 < blocks)
+        def _():
+            load_of(v + 2).start()
+
+        def two_chunks(c, inner):
+            gate(v, 2 * c, 0)
+            gate(v, 2 * c + 1, 1)
+            return inner
+
+        with jax.named_scope("c_gate"):
+            lax.fori_loop(0, chunks // 2, two_chunks, 0)
+        return carry
+
+    def swap_in(v, h, strips=STEP // STRIP):
+        at = pl.ds(pl.multiple_of(v * LANES, LANES), LANES)
+
+        def one_strip(s, inner):
+            rows = pl.ds(pl.multiple_of(s * STRIP, STRIP), STRIP)
+            parts = []
+            for k in range(PACK):
+                here = pl.ds(pl.multiple_of((h * PACK + k) * STEP + s * STRIP, STRIP), STRIP)
+                parts.append(gated[here, at])
+            for g, part in enumerate(by_filter(parts, lane_group)):
+                source[v * PACK + g, rows, h * LANES : (h + 1) * LANES] = part
+            return inner
+
+        lax.fori_loop(0, strips, one_strip, 0)
+
+    smalls[0].wait()
+    lax.fori_loop(0, 2, gate_block, 0)
+    load_weight.start()
+
+    with jax.named_scope("c_smalls"):
+        for copy in smalls[1:]:
+            copy.wait()
     rate_all = rate_in[...]
     scale_all = residue_in[...] * jnp.sqrt(one_less_exp(2.0 * rate_all))
     for f in range(filters):
@@ -204,53 +273,6 @@
         (filters, source.shape[1] - STEP - 3 * MODES, width), BF16
     )
 
-    def gate(v, c, earlier_of):
-        at = pl.ds(pl.multiple_of(v * LANES, LANES), LANES)
-        here = pl.ds(pl.multiple_of(c * STEP, STEP), STEP)
-        parts = []
-        for i in range(3):
-            rows = jnp.concatenate(
-                [earlier_of(i, at).astype(F32), feat[i, here, at].astype(F32)], axis=0
-            )
-            tap = taps[:, i, at]
-            value = (
-                tap[0:1] * rows[RIM:]
-                + tap[1:2] * pltpu.roll(rows, 1, 0)[RIM:]
-                + tap[2:3] * pltpu.roll(rows, 2, 0)[RIM:]
-            )
-            parts.append(value)
-        query[here, at] = parts[0].astype(BF16)
-        gated[here, at] = (parts[1] * parts[2]).astype(BF16)
-
-    def gate_block(v, carry):
-        load_of(v).wait()
-
-        def one_chunk(c, inner):
-            before = pl.ds(pl.multiple_of(c * STEP - RIM, RIM), RIM)
-            gate(v, c, lambda i, at: feat[i, before, at])
-            return inner
-
-        gate(v, 0, lambda i, at: jnp.zeros((RIM, LANES), F32))
-        lax.fori_loop(1, chunks, one_chunk, 0)
-        return carry
-
-    def swap_in(v, h, strips=STEP // STRIP):
-        at = pl.ds(pl.multiple_of(v * LANES, LANES), LANES)
-
-        def one_strip(s, inner):
-            rows = pl.ds(pl.multiple_of(s * STRIP, STRIP), STRIP)
-            parts = []
-            for k in range(PACK):
-                here = pl.ds(pl.multiple_of((h * PACK + k) * STEP + s * STRIP, STRIP), STRIP)
-                parts.append(gated[here, at])
-            for g, part in enumerate(by_filter(parts, lane_group)):
-                source[v * PACK + g, rows, h * LANES : (h + 1) * LANES] = part
-            return inner
-
-        lax.fori_loop(0, strips, one_strip, 0)
-
-    lax.fori_loop(0, blocks // 2, gate_block, 0)
-
     with jax.named_scope("c_barrier"):
         pl.semaphore_wait(barrier, len(greeted))
     rim_copy = pltpu.make_async_remote_copy(
@@ -280,7 +302,7 @@
 
     weight_copy = sent(weight_hbm.at[:, other_cols], weight.at[pl.ds(depth, depth), :], to_core)
 
-    lax.fori_loop(blocks // 2, blocks, gate_block, 0)
+    lax.fori_loop(2, blocks, gate_block, 0)
 
     def state_block(v, carry):
         at = pl.ds(pl.multiple_of(v * LANES, LANES), LANES)
@@ -409,7 +431,18 @@
     with jax.named_scope("c_states"):
         lax.fori_loop(0, blocks, state_rows, 0)
 
-    def block_out(h):
+    def far_pass(v):
+        rows = pl.ds(pl.multiple_of(far * block, block), block)
+        return pltpu.make_async_remote_copy(
+            src_ref=mixed.at[rows, pl.ds(pl.multiple_of(v * LANES, LANES), LANES)],
+            dst_ref=mixed.at[rows, pl.ds(pl.multiple_of(depth + v * LANES, LANES), LANES)],
+            send_sem=pass_send.at[v],
+            recv_sem=pass_recv.at[v],
+            device_id=to_core,
+            device_id_type=MESH,
+        )
+
+    def block_out(h, then=lambda v: None):
         def one_block(v, carry):
             at = pl.ds(pl.multiple_of(v * LANES, LANES), LANES)
             wide = pl.ds(pl.multiple_of(h * LANES, LANES), LANES)
@@ -431,6 +464,7 @@
                 return inner
 
             lax.fori_loop(0, STEP // STRIP, one_strip, 0)
+            then(v)
             return carry
 
         return one_block
@@ -443,26 +477,28 @@
 
     first_half = far // 2
     with jax.named_scope("c_half1"):
-        lax.fori_loop(0, blocks, block_out(first_half), 0)
-    passed = [passed_on(far), passed_on(far + 1 - 2 * lax.rem(far, 2))]
-    lax.fori_loop(0, 1, block_out(1 - first_half), 0)
+        lax.fori_loop(0, blocks, block_out(first_half, lambda v: far_pass(v).start()), 0)
+    passed = [passed_on(far + 1 - 2 * lax.rem(far, 2))]
 
     def tiles(token, rows, first, count, store):
         wide = count // TILE
 
-        def one(n, carry):
-            i, j = n // wide, lax.rem(n, wide)
+        def one(n, carry, whole=True):
+            i, j = (n // wide, lax.rem(n, wide)) if whole else (n, wide)
             r = pl.multiple_of(i * sub, sub)
             c = pl.multiple_of(j * TILE, TILE)
+            size = TILE if whole else count - wide * TILE
             value = jnp.dot(
                 mixed[pl.ds(pl.multiple_of(token + r, sub), sub), :],
-                weight[:, pl.ds(pl.multiple_of(first + c, TILE), TILE)],
+                weight[:, pl.ds(pl.multiple_of(first + c, LANES), size)],
                 preferred_element_type=F32,
             )
-            store(pl.ds(r, sub), pl.ds(c, TILE), value)
+            store(pl.ds(r, sub), pl.ds(c, size), value)
             return carry
 
         lax.fori_loop(0, (rows // sub) * wide, one, 0)
+        if count % TILE:
+            lax.fori_loop(0, rows // sub, lambda n, carry: one(n, carry, False), 0)
 
     def start_of(at):
         return at * block
@@ -477,99 +513,114 @@
 
     mine, others = z * sub, (1 - z) * sub
     order = (far, right, lefts, x)
+    bands = (others, mine)
 
     def z_first(k):
         at = order[k]
-        tiles(start_of(at) + others, sub, half, half, plain(z_send.at[k]))
+        tiles(start_of(at) + others, sub, half, rest, plain(z_send.at[k]))
         return sent(z_send.at[k], z_recv.at[k], to_z)
 
     with jax.named_scope("c_w_start"):
         load_weight.wait()
         weight_copy.wait_recv()
-        passed[0].wait_recv()
-    zs = [z_first(0)]
-    fars = []
-    for s, to in ((0, to_right), (1, to_left)):
-        tiles(start_of(far), block, s * quarter, quarter, plain(far_send.at[s]))
-        fars.append(sent(far_send.at[s], far_recv.at[s], to))
+        for v in range(blocks):
+            far_pass(v).wait_recv()
+    starts, fars = [], ([], [])
+    for part in (0, 1):
+        first, size = z_parts[part]
+        piece = pl.ds(first, size)
+        view = z_send.at[0, :, piece]
+        tiles(start_of(far) + others, sub, half + first, size, plain(view))
+        starts.append(sent(view, z_recv.at[0, :, piece], to_z))
+        for s, to in ((0, to_right), (1, to_left)):
+            first, size = x_parts[s]
+            rows, width = pl.ds(pl.multiple_of(bands[part], sub), sub), pl.ds(0, size)
+            view = far_send.at[s, rows, width]
+            tiles(start_of(far) + bands[part], sub, first, size, plain(view))
+            fars[s].append(sent(view, far_recv.at[s, rows, width], to))
 
     with jax.named_scope("c_half2"):
-        lax.fori_loop(1, blocks, block_out(1 - first_half), 0)
+        lax.fori_loop(0, blocks, block_out(1 - first_half), 0)
     passed += [passed_on(x + 1 - 2 * lax.rem(x, 2)), passed_on(x)]
     with jax.named_scope("c_w_passed"):
-        for copy in passed[1:]:
+        for copy in passed:
             copy.wait_recv()
-    zs.append(z_first(1))
+    zs = [None, z_first(1)]
     sides = ((0, right, to_right), (1, lefts, to_left))
-    nears = {}
+    nears = ([], [])
+
+    def near(s, side, part, at, to):
+        first, size = x_parts[side]
+        rows, width = pl.ds(pl.multiple_of(bands[part], sub), sub), pl.ds(0, size)
+        view = near_send.at[s, side, rows, width]
+        extra = ()
+        if s == side:
+            with jax.named_scope("c_w_far"):
+                fars[s][part].wait_recv()
+            extra = (far_recv.at[s, rows],)
+        tiles(start_of(at) + bands[part], sub, first, size, plain(view, extra))
+        nears[part].append(sent(view, near_recv.at[s, side, rows, width], to))
+
     for s, at, to in sides:
-        side = 1 - s
-        tiles(start_of(at), block, side * quarter, quarter, plain(near_send.at[s, side]))
-        nears[s, side] = sent(near_send.at[s, side], near_recv.at[s, side], to)
+        near(s, 1 - s, 0, at, to)
     zs.append(z_first(2))
+    for s, at, to in sides:
+        near(s, s, 0, at, to)
+    for s, at, to in sides:
+        near(s, 1 - s, 1, at, to)
     zs.append(z_first(3))
+    for s, at, to in sides:
+        near(s, s, 1, at, to)
 
     with jax.named_scope("c_w_z0"):
-        zs[0].wait_recv()
+        for copy in starts:
+            copy.wait_recv()
     fars2 = []
     for s, to in ((0, to_right), (1, to_left)):
-        at = pl.ds(s * quarter, quarter)
+        first, size = z_parts[s]
+        width = pl.ds(0, size)
+        view = far2_send.at[s, :, width]
         tiles(
             start_of(far) + mine,
             sub,
-            half + s * quarter,
-            quarter,
-            plain(far2_send.at[s], (z_recv.at[0, :, at],)),
-        )
-        fars2.append(sent(far2_send.at[s], far2_recv.at[s], to))
-    for s, at, to in sides:
-        with jax.named_scope("c_w_far"):
-            fars[s].wait_recv()
+            half + first,
+            size,
+            plain(view, (z_recv.at[0, :, pl.ds(first, size)],)),
+        )
+        fars2.append(sent(view, far2_recv.at[s, :, width], to))
+
+    nears2 = {}
+
+    def near2(s, side, at, to, extra):
+        first, size = z_parts[side]
+        width = pl.ds(0, size)
+        view = near2_send.at[s, side, :, width]
         tiles(
-            start_of(at), block, s * quarter, quarter, plain(near_send.at[s, s], (far_recv.at[s],))
-        )
-        nears[s, s] = sent(near_send.at[s, s], near_recv.at[s, s], to)
-
-    nears2 = {}
+            start_of(at) + mine,
+            sub,
+            half + first,
+            size,
+            plain(view, (z_recv.at[1 + s, :, pl.ds(first, size)],) + extra),
+        )
+        nears2[s, side] = sent(view, near2_recv.at[s, side, :, width], to)
+
     for s, at, to in sides:
         with jax.named_scope("c_w_z12"):
             zs[1 + s].wait_recv()
-        side = 1 - s
-        piece = pl.ds(side * quarter, quarter)
-        tiles(
-            start_of(at) + mine,
-            sub,
-            half + side * quarter,
-            quarter,
-            plain(near2_send.at[s, side], (z_recv.at[1 + s, :, piece],)),
-        )
-        nears2[s, side] = sent(near2_send.at[s, side], near2_recv.at[s, side], to)
-    for s, at, to in sides:
-        with jax.named_scope("c_w_far2"):
-            fars2[s].wait_recv()
-        piece = pl.ds(s * quarter, quarter)
-        tiles(
-            start_of(at) + mine,
-            sub,
-            half + s * quarter,
-            quarter,
-            plain(near2_send.at[s, s], (z_recv.at[1 + s, :, piece], far2_recv.at[s])),
-        )
-        nears2[s, s] = sent(near2_send.at[s, s], near2_recv.at[s, s], to)
-
+        near2(s, 1 - s, at, to, ())
     with jax.named_scope("c_w_near"):
-        for copy in nears.values():
+        for copy in nears[0]:
             copy.wait_recv()
     for side in (0, 1):
-        piece = pl.ds(side * quarter, quarter)
+        first, size = x_parts[side]
         away = pl.ds(pl.multiple_of(others, sub), sub)
         tiles(
             start_of(x) + others,
             sub,
-            side * quarter,
-            quarter,
+            first,
+            size,
             plain(
-                turn_send.at[:, piece],
+                turn_send.at[:, pl.ds(first, size)],
                 (near_recv.at[0, side, away], near_recv.at[1, side, away]),
             ),
         )
@@ -580,69 +631,81 @@
         sent(turn_send.at[my_rows], turn_recv.at[0], to_z),
     ]
 
+    for s, at, to in sides:
+        with jax.named_scope("c_w_far2"):
+            fars2[s].wait_recv()
+        near2(s, s, at, to, (far2_recv.at[s],))
+
     def kept(offset, extra):
         def store(r, c, value):
             for e in extra:
                 value = value + e[r, c].astype(F32)
-            held[r, pl.ds(pl.multiple_of(offset + c.start, TILE), TILE)] = value
+            held[r, pl.ds(pl.multiple_of(offset + c.start, LANES), c.size)] = value
 
         return store
 
+    with jax.named_scope("c_w_near1"):
+        for copy in nears[1]:
+            copy.wait_recv()
     for side in (0, 1):
+        first, size = x_parts[side]
         here = pl.ds(pl.multiple_of(mine, sub), sub)
         tiles(
             start_of(x) + mine,
             sub,
-            side * quarter,
-            quarter,
-            kept(side * quarter, (near_recv.at[0, side, here], near_recv.at[1, side, here])),
-        )
-    first = pl.ds(0, half)
-    last_send[0] = held[other_rows, first].astype(BF16)
-    lasts = [sent(last_send.at[0], last_recv.at[0], to_core)]
+            first,
+            size,
+            kept(first, (near_recv.at[0, side, here], near_recv.at[1, side, here])),
+        )
+    x_cols = pl.ds(0, half)
+    last_x_send[...] = held[other_rows, x_cols].astype(BF16)
+    last_x = sent(last_x_send, last_x_recv, to_core)
     with jax.named_scope("c_w_z3"):
         zs[3].wait_recv()
     for side in (0, 1):
-        piece = pl.ds(side * quarter, quarter)
+        first, size = z_parts[side]
         tiles(
             start_of(x) + mine,
             sub,
-            half + side * quarter,
-            quarter,
-            kept(half + side * quarter, (z_recv.at[3, :, piece],)),
+            half + first,
+            size,
+            kept(half + first, (z_recv.at[3, :, pl.ds(first, size)],)),
         )
     my_first = pl.multiple_of(core * cols, cols)
+    other_first = pl.multiple_of((1 - core) * cols, cols)
     with jax.named_scope("c_w_near2"):
         for copy in nears2.values():
             copy.wait_recv()
     for rows, keep in ((other_rows, False), (my_rows, True)):
         for side in (0, 1):
-            at = pl.ds(half + side * quarter, quarter)
+            first, size = z_parts[side]
             value = (
-                held[rows, at]
-                + near2_recv[0, side, rows, :].astype(F32)
-                + near2_recv[1, side, rows, :].astype(F32)
+                held[rows, pl.ds(half + first, size)]
+                + near2_recv[0, side, rows, :size].astype(F32)
+                + near2_recv[1, side, rows, :size].astype(F32)
             ).astype(BF16)
             if keep:
-                out_ref[:, pl.ds(my_first + half + side * quarter, quarter)] = value
+                out_ref[:, pl.ds(pl.multiple_of(my_first + half + first, LANES), size)] = value
             else:
-                last_send[1, :, side * quarter : (side + 1) * quarter] = value
+                last_z_send[:, first : first + size] = value
         if not keep:
-            lasts.append(sent(last_send.at[1], last_recv.at[1], to_core))
-    other_first = pl.multiple_of((1 - core) * cols, cols)
-    with jax.named_scope("c_w_last"):
-        lasts[1].wait_recv()
-    out_ref[:, pl.ds(other_first + half, half)] = last_recv[1]
+            last_z = sent(last_z_send, last_z_recv, to_core)
     with jax.named_scope("c_w_turn"):
-        lasts[0].wait_recv()
+        last_x.wait_recv()
         turns[0].wait_recv()
     out_ref[:, pl.ds(other_first, half)] = (
-        last_recv[0].astype(F32) + turn_recv[1].astype(F32)
+        last_x_recv[...].astype(F32) + turn_recv[1].astype(F32)
     ).astype(BF16)
-    turns[1].wait_recv()
+    with jax.named_scope("c_w_turn2"):
+        turns[1].wait_recv()
     out_ref[:, pl.ds(my_first, half)] = (
-        held[my_rows, first] + turn_recv[0].astype(F32)
+        held[my_rows, x_cols] + turn_recv[0].astype(F32)
     ).astype(BF16)
+    with jax.named_scope("c_w_last"):
+        last_z.wait_recv()
+    out_ref[:, pl.ds(pl.multiple_of(other_first + half, LANES), rest)] = last_z_recv[...]
+    for v in range(blocks):
+        far_pass(v).wait_send()
     for copy in used:
         copy.wait_send()
 
@@ -655,16 +718,19 @@
     width = chunks * GROUP
     outs = weight.shape[1]
     cols = outs // 2
-    half, quarter = cols // 2, cols // 4
+    half, x_parts, z_parts = column_parts(cols)
+    rest = cols - half
+    x_most = max(size for _, size in x_parts)
+    z_most = max(size for _, size in z_parts)
     block = tokens // 4
     sub = block // 2
     own = sub // 2
     pairs = [
-        (4, sub, half),
-        (2, block, quarter),
-        (2, 2, block, quarter),
-        (2, sub, quarter),
-        (2, 2, sub, quarter),
+        (4, sub, rest),
+        (2, block, x_most),
+        (2, 2, block, x_most),
+        (2, sub, z_most),
+        (2, 2, sub, z_most),
     ]
     return pl.pallas_call(
         kernel,
@@ -684,6 +750,7 @@
             pltpu.VMEM((filters, MODES, LANES), F32),
             pltpu.VMEM((filters, MODES, LANES), F32),
             pltpu.VMEM((3, RIM, channels), BF16),
+            pltpu.VMEM((2, 3, RIM + STEP, LANES), F32),
             pltpu.VMEM((tokens, channels), BF16),
             pltpu.VMEM((tokens, channels), BF16),
             pltpu.VMEM((filters, 2 * STEP, width), BF16),
@@ -702,8 +769,12 @@
             pltpu.VMEM((sub, half), BF16),
             pltpu.VMEM((2, own, half), BF16),
             pltpu.VMEM((sub, cols), F32),
-            pltpu.VMEM((2, own, half), BF16),
-            pltpu.VMEM((2, own, half), BF16),
+            pltpu.VMEM((own, half), BF16),
+            pltpu.VMEM((own, half), BF16),
+            pltpu.VMEM((own, rest), BF16),
+            pltpu.VMEM((own, rest), BF16),
+            pltpu.SemaphoreType.DMA((channels // LANES,)),
+            pltpu.SemaphoreType.DMA((channels // LANES,)),
             pltpu.SemaphoreType.DMA((4,)),
             pltpu.SemaphoreType.DMA((channels // LANES + 1,)),
             pltpu.SemaphoreType.DMA((2,)),

time: 88.9 us -> 85.9 us (0.966)
  Pallas kernels: 87.8 us -> 84.8 us
    pallas_call x1, Pallas kernels: 87.8 us -> 84.8 us  [on_device(): pl.pallas_call(kernel, out_shape=jax.ShapeDtypeStruct((own, outs), BF16),...]
where the time goes in v4:
time: 85.9 us; the launch traced here: 85.8 us
  Pallas kernels  84.8 us (99%)
  local copies, waits for them, and re-layouts  0.97 us (1%)
    pallas_call x1, Pallas kernels, on_device(): pl.pallas_call(kernel, out_shape=jax.ShapeDtypeStruct((own, outs), BF16),...  84.8 us

profile of v4, /device:TPU:1, one launch (start us, length us, event | category | flops | bytes accessed | tf_op | source)
XLA Modules:
  0.0 85.8 jit_solution(7668699438891334519)
XLA Ops:
  0.0 84.8 %hyena.1 = bf16[128,4096]{1,0:T(8,128)(2,1)S(1)} custom-call(bf16[3,2048,512]{2,1,0:T(8,128)(2,1)} %bitcast.3, f32[3,3,512]{2,1,0:T(4,128)} %taps_hbm.1, f32[16,32]{1,0:T(8,128)} %bitcast.4, f32[16,32]{1,0:T(8,128)} %bitcast.5, f32[512]{0:T(512)} %skip_hbm.1, bf16[512,4096]{1,0:T(8,128)(2,1)} %weight_hbm.1), custom_call_target="tpu_custom_call" | custom-call | tf_op jit(solution)/shard_map/hyena/pallas_call | solution.py:735
  84.8 1.0 %copy.8 = bf16[128,4096]{1,0:T(8,128)(2,1)} copy(bf16[128,4096]{1,0:T(8,128)(2,1)S(1)} %hyena.1) | data formatting | bytes 2097152

commit v5 on v4

--- a/solution.py
+++ b/solution.py
@@ -13,12 +13,13 @@
 BF16 = jnp.bfloat16
 LANES = 128
 TILE = 256
-COPIES = 31
+COPIES = 33
+UNROLL = 4
 STEP = 128
 GROUP = 16
 PACK = LANES // GROUP
 MODES = 16
-STRIP = 64
+STRIP = 32
 RIM = 16
 
 
@@ -104,6 +105,7 @@
     chan_rates,
     amend,
     total,
+    passed_total,
     totals,
     result,
     mixed,
@@ -118,6 +120,7 @@
     far2_recv,
     near2_send,
     near2_recv,
+    cross_recv,
     turn_send,
     turn_recv,
     held,
@@ -183,9 +186,12 @@
         weight_hbm.at[:, my_cols], weight.at[pl.ds(0, depth), :], load_sem.at[blocks]
     )
 
+    rim[...] = jnp.zeros_like(rim)
+    totals[...] = jnp.zeros_like(totals)
     barrier = pltpu.get_barrier_semaphore()
     greeted = [{"ctx": lax.rem(ctx + d, peers)} for d in range(1, peers)]
     greeted += [to_right, to_left, to_z, to_core, to_both]
+    greeted += [{"chan_0": right, "chan_2": 1 - core}, {"chan_0": lefts, "chan_2": 1 - core}]
     for to in greeted:
         pl.semaphore_signal(barrier, inc=1, device_id=to, device_id_type=MESH)
 
@@ -225,13 +231,13 @@
         def _():
             load_of(v + 2).start()
 
-        def two_chunks(c, inner):
-            gate(v, 2 * c, 0)
-            gate(v, 2 * c + 1, 1)
+        def some_chunks(c, inner):
+            for k in range(UNROLL):
+                gate(v, UNROLL * c + k, k)
             return inner
 
         with jax.named_scope("c_gate"):
-            lax.fori_loop(0, chunks // 2, two_chunks, 0)
+            lax.fori_loop(0, chunks // UNROLL, some_chunks, 0)
         return carry
 
     def swap_in(v, h, strips=STEP // STRIP):
@@ -247,7 +253,8 @@
                 source[v * PACK + g, rows, h * LANES : (h + 1) * LANES] = part
             return inner
 
-        lax.fori_loop(0, strips, one_strip, 0)
+        for s in range(strips):
+            one_strip(s, 0)
 
     smalls[0].wait()
     lax.fori_loop(0, 2, gate_block, 0)
@@ -283,7 +290,11 @@
         device_id={"ctx": lax.rem(ctx + 1, peers)},
         device_id_type=MESH,
     )
-    rim_copy.start()
+
+    @pl.when(ctx < peers - 1)
+    def _():
+        rim_copy.start()
+
     used = []
 
     def sent(src, dst, to):
@@ -364,23 +375,37 @@
         return carry
 
     with jax.named_scope("c_rim"):
-        rim_copy.wait()
+
+        @pl.when(ctx > 0)
+        def _():
+            rim_copy.wait_recv()
+
     lax.fori_loop(0, blocks, amend_block, 0)
 
-    sums = []
-    for d in range(1, peers):
-        copy = pltpu.make_async_remote_copy(
-            src_ref=total,
+    passed_total[...] = total[...].astype(BF16)
+
+    def sum_copy(d):
+        return pltpu.make_async_remote_copy(
+            src_ref=passed_total,
             dst_ref=totals.at[d - 1],
             send_sem=sum_send.at[d - 1],
             recv_sem=sum_recv.at[d - 1],
             device_id={"ctx": lax.rem(ctx + d, peers)},
             device_id_type=MESH,
         )
-        copy.start()
-        sums.append(copy)
-
-    def build(f, carry):
+
+    for d in range(1, peers):
+
+        @pl.when(ctx + d < peers)
+        def _():
+            sum_copy(d).start()
+
+    def build(n, carry):
+        for k in range(UNROLL):
+            build_one(UNROLL * n + k)
+        return carry
+
+    def build_one(f):
         first = jnp.sum(scales[f] * jnp.exp(-rates[f] * back), axis=0, keepdims=True)
         turned = pltpu.roll(
             jnp.broadcast_to(first, (STEP, LANES)), 0, 1, stride=1, stride_axis=0
@@ -389,7 +414,6 @@
         hi, lo = hi_lo(scale_row[pl.ds(f, 1), :] * jnp.exp(-rate_row[pl.ds(f, 1), :] * after))
         second = (col >= MODES) & (col < 2 * MODES)
         left[f, :, LANES:] = jnp.where(second, lo, hi).astype(BF16)
-        return carry
 
     def swap_again(v, carry):
         swap_in(v, 0, 1)
@@ -397,17 +421,21 @@
 
     lax.fori_loop(0, blocks, swap_again, 0)
     with jax.named_scope("c_build"):
-        lax.fori_loop(0, filters, build, 0)
+        lax.fori_loop(0, filters // UNROLL, build, 0)
     with jax.named_scope("c_sums"):
-        for copy in sums:
-            copy.wait()
+        for d in range(1, peers):
+
+            @pl.when(ctx >= d)
+            def _():
+                sum_copy(d).wait_recv()
+
     for v in range(blocks):
         at = pl.ds(v * LANES, LANES)
         chan_rate = chan_rates[:, at]
         carried = jnp.zeros((MODES, LANES), F32)
         for d in range(1, peers):
             decay = jnp.exp(chan_rate * (-float((d - 1) * tokens)))
-            carried = carried + jnp.where(ctx >= d, decay * totals[d - 1, :, at], 0.0)
+            carried = carried + jnp.where(ctx >= d, decay * totals[d - 1, :, at].astype(F32), 0.0)
         total[:, at] = carried
 
     def state_rows(v, carry):
@@ -463,7 +491,8 @@
                     mixed[here, at] = (query[here, at].astype(F32) * value).astype(BF16)
                 return inner
 
-            lax.fori_loop(0, STEP // STRIP, one_strip, 0)
+            for s in range(STEP // STRIP):
+                one_strip(s, 0)
             then(v)
             return carry
 
@@ -589,7 +618,9 @@
         )
         fars2.append(sent(view, far2_recv.at[s, :, width], to))
 
-    nears2 = {}
+    my_rows = pl.ds(pl.multiple_of(core * own, own), own)
+    other_rows = pl.ds(pl.multiple_of((1 - core) * own, own), own)
+    nears2, crosses = [], []
 
     def near2(s, side, at, to, extra):
         first, size = z_parts[side]
@@ -602,7 +633,14 @@
             size,
             plain(view, (z_recv.at[1 + s, :, pl.ds(first, size)],) + extra),
         )
-        nears2[s, side] = sent(view, near2_recv.at[s, side, :, width], to)
+        if s != side:
+            nears2.append(sent(view, near2_recv.at[s, side, :, width], to))
+            return
+        view = near2_send.at[s, side, other_rows, width]
+        across = {"chan_0": at, "chan_2": 1 - core}
+        crosses.append(sent(view, cross_recv.at[s, :, width], across))
+        view = near2_send.at[s, side, my_rows, width]
+        crosses.append(sent(view, near2_recv.at[s, side, my_rows, width], to))
 
     for s, at, to in sides:
         with jax.named_scope("c_w_z12"):
@@ -624,8 +662,6 @@
                 (near_recv.at[0, side, away], near_recv.at[1, side, away]),
             ),
         )
-    my_rows = pl.ds(pl.multiple_of(core * own, own), own)
-    other_rows = pl.ds(pl.multiple_of((1 - core) * own, own), own)
     turns = [
         sent(turn_send.at[other_rows], turn_recv.at[1], to_both),
         sent(turn_send.at[my_rows], turn_recv.at[0], to_z),
@@ -674,22 +710,15 @@
     my_first = pl.multiple_of(core * cols, cols)
     other_first = pl.multiple_of((1 - core) * cols, cols)
     with jax.named_scope("c_w_near2"):
-        for copy in nears2.values():
+        for copy in nears2:
             copy.wait_recv()
-    for rows, keep in ((other_rows, False), (my_rows, True)):
-        for side in (0, 1):
-            first, size = z_parts[side]
-            value = (
-                held[rows, pl.ds(half + first, size)]
-                + near2_recv[0, side, rows, :size].astype(F32)
-                + near2_recv[1, side, rows, :size].astype(F32)
-            ).astype(BF16)
-            if keep:
-                out_ref[:, pl.ds(pl.multiple_of(my_first + half + first, LANES), size)] = value
-            else:
-                last_z_send[:, first : first + size] = value
-        if not keep:
-            last_z = sent(last_z_send, last_z_recv, to_core)
+    for side in (0, 1):
+        first, size = z_parts[side]
+        last_z_send[:, first : first + size] = (
+            held[other_rows, pl.ds(half + first, size)]
+            + near2_recv[1 - side, side, other_rows, :size].astype(F32)
+        ).astype(BF16)
+    last_z = sent(last_z_send, last_z_recv, to_core)
     with jax.named_scope("c_w_turn"):
         last_x.wait_recv()
         turns[0].wait_recv()
@@ -703,9 +732,33 @@
     ).astype(BF16)
     with jax.named_scope("c_w_last"):
         last_z.wait_recv()
-    out_ref[:, pl.ds(pl.multiple_of(other_first + half, LANES), rest)] = last_z_recv[...]
+    with jax.named_scope("c_w_cross"):
+        for copy in crosses:
+            copy.wait_recv()
+    for side in (0, 1):
+        first, size = z_parts[side]
+        out_ref[:, pl.ds(pl.multiple_of(my_first + half + first, LANES), size)] = (
+            held[my_rows, pl.ds(half + first, size)]
+            + near2_recv[0, side, my_rows, :size].astype(F32)
+            + near2_recv[1, side, my_rows, :size].astype(F32)
+        ).astype(BF16)
+        out_ref[:, pl.ds(pl.multiple_of(other_first + half + first, LANES), size)] = (
+            last_z_recv[:, first : first + size].astype(F32)
+            + cross_recv[side, :, :size].astype(F32)
+        ).astype(BF16)
     for v in range(blocks):
         far_pass(v).wait_send()
+
+    @pl.when(ctx < peers - 1)
+    def _():
+        rim_copy.wait_send()
+
+    for d in range(1, peers):
+
+        @pl.when(ctx + d < peers)
+        def _():
+            sum_copy(d).wait_send()
+
     for copy in used:
         copy.wait_send()
 
@@ -750,7 +803,7 @@
             pltpu.VMEM((filters, MODES, LANES), F32),
             pltpu.VMEM((filters, MODES, LANES), F32),
             pltpu.VMEM((3, RIM, channels), BF16),
-            pltpu.VMEM((2, 3, RIM + STEP, LANES), F32),
+            pltpu.VMEM((UNROLL, 3, RIM + STEP, LANES), F32),
             pltpu.VMEM((tokens, channels), BF16),
             pltpu.VMEM((tokens, channels), BF16),
             pltpu.VMEM((filters, 2 * STEP, width), BF16),
@@ -759,13 +812,15 @@
             pltpu.VMEM((MODES, channels), F32),
             pltpu.VMEM((MODES, channels), F32),
             pltpu.VMEM((MODES, channels), F32),
-            pltpu.VMEM((peers - 1, MODES, channels), F32),
+            pltpu.VMEM((MODES, channels), BF16),
+            pltpu.VMEM((peers - 1, MODES, channels), BF16),
             pltpu.VMEM((PACK, STEP, LANES), BF16),
             pltpu.VMEM((tokens, 2 * channels), BF16),
             pltpu.VMEM((2 * channels, cols), BF16),
         ]
         + [pltpu.VMEM(shape, BF16) for shape in pairs for _ in range(2)]
         + [
+            pltpu.VMEM((2, own, z_most), BF16),
             pltpu.VMEM((sub, half), BF16),
             pltpu.VMEM((2, own, half), BF16),
             pltpu.VMEM((sub, cols), F32),

time: 85.9 us -> 79.3 us (0.923)
  Pallas kernels: 84.8 us -> 77.8 us
    pallas_call x1, Pallas kernels: 84.8 us -> 77.8 us  [on_device(): pl.pallas_call(kernel, out_shape=jax.ShapeDtypeStruct((own, outs), BF16),...]
where the time goes in v5:
time: 79.3 us; the launch traced here: 78.8 us
  Pallas kernels  77.8 us (98%)
  local copies, waits for them, and re-layouts  0.97 us (1%)
    pallas_call x1, Pallas kernels, on_device(): pl.pallas_call(kernel, out_shape=jax.ShapeDtypeStruct((own, outs), BF16),...  77.8 us

profile of v5, /device:TPU:1, one launch (start us, length us, event | category | flops | bytes accessed | tf_op | source)
XLA Modules:
  0.0 78.8 jit_solution(6925611581860005857)
XLA Ops:
  0.0 77.8 %hyena.1 = bf16[128,4096]{1,0:T(8,128)(2,1)S(1)} custom-call(bf16[3,2048,512]{2,1,0:T(8,128)(2,1)} %bitcast.3, f32[3,3,512]{2,1,0:T(4,128)} %taps_hbm.1, f32[16,32]{1,0:T(8,128)} %bitcast.4, f32[16,32]{1,0:T(8,128)} %bitcast.5, f32[512]{0:T(512)} %skip_hbm.1, bf16[512,4096]{1,0:T(8,128)(2,1)} %weight_hbm.1), custom_call_target="tpu_custom_call" | custom-call | tf_op jit(solution)/shard_map/hyena/pallas_call | solution.py:788
  77.8 1.0 %copy.8 = bf16[128,4096]{1,0:T(8,128)(2,1)} copy(bf16[128,4096]{1,0:T(8,128)(2,1)S(1)} %hyena.1) | data formatting | bytes 2097152

commit v6 on v5

--- a/solution.py
+++ b/solution.py
@@ -204,25 +204,39 @@
     back = lax.rem(STEP - lane_mode, STEP).astype(F32)
     ahead = (STEP - 1 - lane_mode).astype(F32)
 
+    def shortened(i, v, c, slot, outside):
+        at = pl.ds(pl.multiple_of(v * LANES, LANES), LANES)
+        here = pl.ds(pl.multiple_of(c * STEP, STEP), STEP)
+        before = pl.ds(pl.multiple_of(jnp.maximum(c * STEP - RIM, 0), RIM), RIM)
+        now = feat[i, here, at].astype(F32)
+        shifts[slot, i, :RIM] = jnp.where(c > 0, feat[i, before, at].astype(F32), outside)
+        shifts[slot, i, RIM:] = now
+        tap = taps[:, i, at]
+        return (
+            tap[0:1] * now
+            + tap[1:2] * shifts[slot, i, RIM - 1 : RIM - 1 + STEP]
+            + tap[2:3] * shifts[slot, i, RIM - 2 : RIM - 2 + STEP]
+        )
+
     def gate(v, c, slot):
         at = pl.ds(pl.multiple_of(v * LANES, LANES), LANES)
         here = pl.ds(pl.multiple_of(c * STEP, STEP), STEP)
-        before = pl.ds(pl.multiple_of(jnp.maximum(c * STEP - RIM, 0), RIM), RIM)
-        parts = []
-        for i in range(3):
-            earlier = feat[i, before, at].astype(F32)
-            now = feat[i, here, at].astype(F32)
-            shifts[slot, i, :RIM] = jnp.where(c > 0, earlier, 0.0)
-            shifts[slot, i, RIM:] = now
-            tap = taps[:, i, at]
-            value = (
-                tap[0:1] * now
-                + tap[1:2] * shifts[slot, i, RIM - 1 : RIM - 1 + STEP]
-                + tap[2:3] * shifts[slot, i, RIM - 2 : RIM - 2 + STEP]
-            )
-            parts.append(value)
-        query[here, at] = parts[0].astype(BF16)
-        gated[here, at] = (parts[1] * parts[2]).astype(BF16)
+        key = shortened(1, v, c, slot, 0.0)
+        gated[here, at] = (key * shortened(2, v, c, slot, 0.0)).astype(BF16)
+
+    def query_block(v, carry):
+        at = pl.ds(pl.multiple_of(v * LANES, LANES), LANES)
+
+        def some_chunks(n, inner):
+            for k in range(UNROLL):
+                c = UNROLL * n + k
+                here = pl.ds(pl.multiple_of(c * STEP, STEP), STEP)
+                value = shortened(0, v, c, k, rim[0, :, at].astype(F32))
+                query[here, at] = value.astype(BF16)
+            return inner
+
+        lax.fori_loop(0, chunks // UNROLL, some_chunks, 0)
+        return carry
 
     def gate_block(v, carry):
         load_of(v).wait()
@@ -344,7 +358,7 @@
     def amend_block(v, carry):
         at = pl.ds(pl.multiple_of(v * LANES, LANES), LANES)
         parts = []
-        for i in range(3):
+        for i in (1, 2):
             rows = jnp.concatenate([rim[i, :, at], feat[i, :RIM, at]], axis=0).astype(F32)
             tap = taps[:, i, at]
             value = (
@@ -355,9 +369,8 @@
             parts.append(value)
         new = (lax.broadcasted_iota(jnp.int32, (RIM, LANES), 0) < 2) & (ctx > 0)
         was = gated[:RIM, at].astype(F32)
-        now = jnp.where(new, (parts[1] * parts[2]).astype(BF16).astype(F32), was)
+        now = jnp.where(new, (parts[0] * parts[1]).astype(BF16).astype(F32), was)
         gated[:RIM, at] = now.astype(BF16)
-        query[:RIM, at] = jnp.where(new, parts[0], query[:RIM, at].astype(F32)).astype(BF16)
         change = now - was
         rate = rates[v * PACK]
         for g in range(1, PACK):
@@ -420,6 +433,8 @@
         return carry
 
     lax.fori_loop(0, blocks, swap_again, 0)
+    with jax.named_scope("c_query"):
+        lax.fori_loop(0, blocks, query_block, 0)
     with jax.named_scope("c_build"):
         lax.fori_loop(0, filters // UNROLL, build, 0)
     with jax.named_scope("c_sums"):
@@ -556,17 +571,17 @@
             far_pass(v).wait_recv()
     starts, fars = [], ([], [])
     for part in (0, 1):
-        first, size = z_parts[part]
-        piece = pl.ds(first, size)
-        view = z_send.at[0, :, piece]
-        tiles(start_of(far) + others, sub, half + first, size, plain(view))
-        starts.append(sent(view, z_recv.at[0, :, piece], to_z))
         for s, to in ((0, to_right), (1, to_left)):
             first, size = x_parts[s]
             rows, width = pl.ds(pl.multiple_of(bands[part], sub), sub), pl.ds(0, size)
             view = far_send.at[s, rows, width]
             tiles(start_of(far) + bands[part], sub, first, size, plain(view))
             fars[s].append(sent(view, far_recv.at[s, rows, width], to))
+        first, size = z_parts[part]
+        piece = pl.ds(first, size)
+        view = z_send.at[0, :, piece]
+        tiles(start_of(far) + others, sub, half + first, size, plain(view))
+        starts.append(sent(view, z_recv.at[0, :, piece], to_z))
 
     with jax.named_scope("c_half2"):
         lax.fori_loop(0, blocks, block_out(1 - first_half), 0)
@@ -595,12 +610,6 @@
     zs.append(z_first(2))
     for s, at, to in sides:
         near(s, s, 0, at, to)
-    for s, at, to in sides:
-        near(s, 1 - s, 1, at, to)
-    zs.append(z_first(3))
-    for s, at, to in sides:
-        near(s, s, 1, at, to)
-
     with jax.named_scope("c_w_z0"):
         for copy in starts:
             copy.wait_recv()
@@ -618,6 +627,12 @@
         )
         fars2.append(sent(view, far2_recv.at[s, :, width], to))
 
+    for s, at, to in sides:
+        near(s, 1 - s, 1, at, to)
+    zs.append(z_first(3))
+    for s, at, to in sides:
+        near(s, s, 1, at, to)
+
     my_rows = pl.ds(pl.multiple_of(core * own, own), own)
     other_rows = pl.ds(pl.multiple_of((1 - core) * own, own), own)
     nears2, crosses = [], []
@@ -646,6 +661,11 @@
         with jax.named_scope("c_w_z12"):
             zs[1 + s].wait_recv()
         near2(s, 1 - s, at, to, ())
+    for s, at, to in sides:
+        with jax.named_scope("c_w_far2"):
+            fars2[s].wait_recv()
+        near2(s, s, at, to, (far2_recv.at[s],))
+
     with jax.named_scope("c_w_near"):
         for copy in nears[0]:
             copy.wait_recv()
@@ -667,11 +687,6 @@
         sent(turn_send.at[my_rows], turn_recv.at[0], to_z),
     ]
 
-    for s, at, to in sides:
-        with jax.named_scope("c_w_far2"):
-            fars2[s].wait_recv()
-        near2(s, s, at, to, (far2_recv.at[s],))
-
     def kept(offset, extra):
         def store(r, c, value):
             for e in extra:
@@ -718,6 +733,10 @@
             held[other_rows, pl.ds(half + first, size)]
             + near2_recv[1 - side, side, other_rows, :size].astype(F32)
         ).astype(BF16)
+        held[my_rows, pl.ds(half + first, size)] = (
+            held[my_rows, pl.ds(half + first, size)]
+            + near2_recv[1 - side, side, my_rows, :size].astype(F32)
+        )
     last_z = sent(last_z_send, last_z_recv, to_core)
     with jax.named_scope("c_w_turn"):
         last_x.wait_recv()
@@ -739,8 +758,7 @@
         first, size = z_parts[side]
         out_ref[:, pl.ds(pl.multiple_of(my_first + half + first, LANES), size)] = (
             held[my_rows, pl.ds(half + first, size)]
-            + near2_recv[0, side, my_rows, :size].astype(F32)
-            + near2_recv[1, side, my_rows, :size].astype(F32)
+            + near2_recv[side, side, my_rows, :size].astype(F32)
         ).astype(BF16)
         out_ref[:, pl.ds(pl.multiple_of(other_first + half + first, LANES), size)] = (
             last_z_recv[:, first : first + size].astype(F32)

time: 79.3 us -> 79.2 us (level)
  no operation moved by 1% of the time
where the time goes in v6:
time: 79.2 us; the launch traced here: 79.1 us
  Pallas kernels  78.1 us (99%)
  local copies, waits for them, and re-layouts  0.97 us (1%)
    pallas_call x1, Pallas kernels, on_device(): pl.pallas_call(kernel, out_shape=jax.ShapeDtypeStruct((own, outs), BF16),...  78.1 us

profile of v6, /device:TPU:1, one launch (start us, length us, event | category | flops | bytes accessed | tf_op | source)
XLA Modules:
  0.0 79.1 jit_solution(944073977530478597)
XLA Ops:
  0.0 78.1 %hyena.1 = bf16[128,4096]{1,0:T(8,128)(2,1)S(1)} custom-call(bf16[3,2048,512]{2,1,0:T(8,128)(2,1)} %bitcast.3, f32[3,3,512]{2,1,0:T(4,128)} %taps_hbm.1, f32[16,32]{1,0:T(8,128)} %bitcast.4, f32[16,32]{1,0:T(8,128)} %bitcast.5, f32[512]{0:T(512)} %skip_hbm.1, bf16[512,4096]{1,0:T(8,128)(2,1)} %weight_hbm.1), custom_call_target="tpu_custom_call" | custom-call | tf_op jit(solution)/shard_map/hyena/pallas_call | solution.py:806
  78.1 1.0 %copy.8 = bf16[128,4096]{1,0:T(8,128)(2,1)} copy(bf16[128,4096]{1,0:T(8,128)(2,1)S(1)} %hyena.1) | data formatting | bytes 2097152

commit v7 on v5

--- a/solution.py
+++ b/solution.py
@@ -556,17 +556,17 @@
             far_pass(v).wait_recv()
     starts, fars = [], ([], [])
     for part in (0, 1):
-        first, size = z_parts[part]
-        piece = pl.ds(first, size)
-        view = z_send.at[0, :, piece]
-        tiles(start_of(far) + others, sub, half + first, size, plain(view))
-        starts.append(sent(view, z_recv.at[0, :, piece], to_z))
         for s, to in ((0, to_right), (1, to_left)):
             first, size = x_parts[s]
             rows, width = pl.ds(pl.multiple_of(bands[part], sub), sub), pl.ds(0, size)
             view = far_send.at[s, rows, width]
             tiles(start_of(far) + bands[part], sub, first, size, plain(view))
             fars[s].append(sent(view, far_recv.at[s, rows, width], to))
+        first, size = z_parts[part]
+        piece = pl.ds(first, size)
+        view = z_send.at[0, :, piece]
+        tiles(start_of(far) + others, sub, half + first, size, plain(view))
+        starts.append(sent(view, z_recv.at[0, :, piece], to_z))
 
     with jax.named_scope("c_half2"):
         lax.fori_loop(0, blocks, block_out(1 - first_half), 0)
@@ -595,12 +595,6 @@
     zs.append(z_first(2))
     for s, at, to in sides:
         near(s, s, 0, at, to)
-    for s, at, to in sides:
-        near(s, 1 - s, 1, at, to)
-    zs.append(z_first(3))
-    for s, at, to in sides:
-        near(s, s, 1, at, to)
-
     with jax.named_scope("c_w_z0"):
         for copy in starts:
             copy.wait_recv()
@@ -618,6 +612,12 @@
         )
         fars2.append(sent(view, far2_recv.at[s, :, width], to))
 
+    for s, at, to in sides:
+        near(s, 1 - s, 1, at, to)
+    zs.append(z_first(3))
+    for s, at, to in sides:
+        near(s, s, 1, at, to)
+
     my_rows = pl.ds(pl.multiple_of(core * own, own), own)
     other_rows = pl.ds(pl.multiple_of((1 - core) * own, own), own)
     nears2, crosses = [], []
@@ -646,6 +646,11 @@
         with jax.named_scope("c_w_z12"):
             zs[1 + s].wait_recv()
         near2(s, 1 - s, at, to, ())
+    for s, at, to in sides:
+        with jax.named_scope("c_w_far2"):
+            fars2[s].wait_recv()
+        near2(s, s, at, to, (far2_recv.at[s],))
+
     with jax.named_scope("c_w_near"):
         for copy in nears[0]:
             copy.wait_recv()
@@ -667,11 +672,6 @@
         sent(turn_send.at[my_rows], turn_recv.at[0], to_z),
     ]
 
-    for s, at, to in sides:
-        with jax.named_scope("c_w_far2"):
-            fars2[s].wait_recv()
-        near2(s, s, at, to, (far2_recv.at[s],))
-
     def kept(offset, extra):
         def store(r, c, value):
             for e in extra:
@@ -718,6 +718,10 @@
             held[other_rows, pl.ds(half + first, size)]
             + near2_recv[1 - side, side, other_rows, :size].astype(F32)
         ).astype(BF16)
+        held[my_rows, pl.ds(half + first, size)] = (
+            held[my_rows, pl.ds(half + first, size)]
+            + near2_recv[1 - side, side, my_rows, :size].astype(F32)
+        )
     last_z = sent(last_z_send, last_z_recv, to_core)
     with jax.named_scope("c_w_turn"):
         last_x.wait_recv()
@@ -739,8 +743,7 @@
         first, size = z_parts[side]
         out_ref[:, pl.ds(pl.multiple_of(my_first + half + first, LANES), size)] = (
             held[my_rows, pl.ds(half + first, size)]
-            + near2_recv[0, side, my_rows, :size].astype(F32)
-            + near2_recv[1, side, my_rows, :size].astype(F32)
+            + near2_recv[side, side, my_rows, :size].astype(F32)
         ).astype(BF16)
         out_ref[:, pl.ds(pl.multiple_of(other_first + half + first, LANES), size)] = (
             last_z_recv[:, first : first + size].astype(F32)

time: 79.3 us -> 78.8 us (level)
  no operation moved by 1% of the time
where the time goes in v7:
time: 78.8 us; the launch traced here: 78.3 us
  Pallas kernels  77.3 us (98%)
  local copies, waits for them, and re-layouts  0.97 us (1%)
    pallas_call x1, Pallas kernels, on_device(): pl.pallas_call(kernel, out_shape=jax.ShapeDtypeStruct((own, outs), BF16),...  77.3 us

profile of v7, /device:TPU:1, one launch (start us, length us, event | category | flops | bytes accessed | tf_op | source)
XLA Modules:
  0.0 78.3 jit_solution(11915269630502039946)
XLA Ops:
  0.0 77.3 %hyena.1 = bf16[128,4096]{1,0:T(8,128)(2,1)S(1)} custom-call(bf16[3,2048,512]{2,1,0:T(8,128)(2,1)} %bitcast.3, f32[3,3,512]{2,1,0:T(4,128)} %taps_hbm.1, f32[16,32]{1,0:T(8,128)} %bitcast.4, f32[16,32]{1,0:T(8,128)} %bitcast.5, f32[512]{0:T(512)} %skip_hbm.1, bf16[512,4096]{1,0:T(8,128)(2,1)} %weight_hbm.1), custom_call_target="tpu_custom_call" | custom-call | tf_op jit(solution)/shard_map/hyena/pallas_call | solution.py:791
  77.3 1.0 %copy.8 = bf16[128,4096]{1,0:T(8,128)(2,1)} copy(bf16[128,4096]{1,0:T(8,128)(2,1)S(1)} %hyena.1) | data formatting | bytes 2097152
